TPU v7x, 256 devices: a whole 4x4x8 slice. The times are simulated.
256 devices in a mesh: events: 8 (over x, z_lo), shells: 32 (over y, z_hi, core).
Axes of the slice: x: 4, y: 4, z: 8 (z_hi: 4, z_lo: 2; z = z_hi * 2 + z_lo), core: 2. Of those that a mesh axis runs over, the one named last changes fastest.
Arguments:
- model: bfloat16 [2097152], P('shells'), may hold values from -6 to 6
- sensitivity: bfloat16 [131072, 64, 128], P(('events', 'shells')), may hold values from -0.1875 to 0.1875
- pick_block: int32 [131072], P(('events', 'shells')), may hold values from 0 to 2047, as said below
- cell_block: int32 [131072], P(('events', 'shells')), may hold values from 0 to 511
- blk_count: int32 [256], P(('events', 'shells')), may hold values from 128 to 512, as said below
- observed: float32 [1048576], P(('events', 'shells')), may hold values from -6 to 6
- pick_weight: float32 [1048576], P(('events', 'shells')), may hold values from 0.2 to 15
- station: int32 [1048576], P(('events', 'shells')), may hold values from 0 to 2047
Outputs:
- gradient: float32 [2097152], P('shells')
- correction: float32 [2048], replicated
- weighted: float32 [1048576], P(('events', 'shells'))
Inputs may be any that keep to these rules, and one draw needn't show every extreme that they name: `blk_count`: each device uses its first slots; some device uses all 512 in every draw. The owner of a slot is pick_block // 64. Among the used slots of one device, at most 32 have one owner; in every event group some owner gets exactly 32 from every device of the group.
All inputs are finite; a program needn't handle non-finite values.
Results may differ from a plain program's by a relative error of at most 0.0026.
Values may be sent and summed in bfloat16 or wider, within the bound.
No kernel may reach another device: no remote copies, remote signals or barrier semaphores. Data moves between devices by JAX's collectives and lax.ppermute only.
A program may use at most 64 MiB of HBM per device.

v0:
```python
import jax
import jax.numpy as jnp
from jax import lax
from jax.sharding import PartitionSpec as P

PICK_BLK = 64
CELL_BLK = 128
STATIONS = 2048


def local(model, sensitivity, pick_block, cell_block, blk_count, observed, pick_weight, station):
    slot_count = blk_count[0]
    slot_total = sensitivity.shape[0]
    slot_step = min(32, slot_total)
    model_rows = model.reshape(-1, CELL_BLK)
    owned_picks = observed.shape[0]
    owned_blocks = owned_picks // PICK_BLK
    shell_count = lax.axis_size("shells")
    group_rows = owned_blocks * shell_count
    turns = (slot_count + slot_step - 1) // slot_step

    def slot_range(turn):
        offset = turn * slot_step
        blocks = lax.dynamic_slice_in_dim(sensitivity, offset, slot_step, 0)
        picks_of = lax.dynamic_slice_in_dim(pick_block, offset, slot_step, 0)
        cells_of = lax.dynamic_slice_in_dim(cell_block, offset, slot_step, 0)
        alive = offset + jnp.arange(slot_step, dtype=jnp.int32) < slot_count
        return (blocks, picks_of, cells_of, alive)

    def slot_values(turn):
        blocks, picks_of, cells_of, alive = slot_range(turn)
        values = jnp.einsum(
            "kpc,kc->kp", blocks, model_rows[cells_of], preferred_element_type=jnp.float32
        )
        return (jnp.where(alive[:, None], values, 0.0), picks_of)

    def forward_turn(turn, partials):
        values, picks_of = slot_values(turn)
        return partials.at[picks_of].add(values)

    partials = lax.fori_loop(0, turns, forward_turn, jnp.zeros((group_rows, PICK_BLK), jnp.float32))
    flat_terms = partials.reshape(-1)
    summed = lax.psum(flat_terms, "shells")
    predicted = lax.dynamic_slice_in_dim(
        summed, lax.axis_index("shells") * owned_picks, owned_picks, 0
    )
    misfit = observed - predicted
    numer_local = jax.ops.segment_sum(pick_weight * misfit, station, num_segments=STATIONS)
    denom_local = jax.ops.segment_sum(pick_weight, station, num_segments=STATIONS)
    numer, denom = lax.psum((numer_local, denom_local), ("events", "shells"))
    correction = numer / (denom + 1.0)
    weighted = pick_weight * (misfit - correction[station])
    weighted_half = weighted.astype(jnp.bfloat16)
    group_resid = lax.all_gather(weighted_half, "shells", axis=0, tiled=True).reshape(
        group_rows, PICK_BLK
    )

    def backward_turn(turn, grads):
        blocks, picks_of, cells_of, alive = slot_range(turn)
        terms = jnp.einsum(
            "kpc,kp->kc", blocks, group_resid[picks_of], preferred_element_type=jnp.float32
        )
        terms = jnp.where(alive[:, None], terms, 0.0)
        return grads.at[cells_of].add(terms)

    grads = lax.fori_loop(0, turns, backward_turn, jnp.zeros(model_rows.shape, jnp.float32))
    gradient = lax.psum(grads.reshape(-1), "events")
    return (gradient, correction, weighted)


def solution(mesh):
    placed = (
        P("shells"),
        P(("events", "shells"), None, None),
        P(("events", "shells")),
        P(("events", "shells")),
        P(("events", "shells")),
        P(("events", "shells")),
        P(("events", "shells")),
        P(("events", "shells")),
    )
    return jax.shard_map(
        local,
        mesh=mesh,
        in_specs=placed,
        out_specs=(P("shells"), P(), P(("events", "shells"))),
        check_vma=False,
    )
```

profile of v0, /device:TPU:1, one launch (start us, length us, event | category | flops | bytes accessed | tf_op | source)
XLA Modules:
  0.0 697.5 jit_solution(82583176409720336)
XLA Ops:
  8.0 61.8 %while.20 = (s32[]{:T(128)}, f32[2048,64]{1,0:T(8,128)S(1)}, s32[]{:T(128)}, s32[512]{0:T(512)}, s32[]{:T(128)}, /*index=5*/bf16[512,64,128]{2,1,0:T(8,128)(2,1)...) while((s32[]{:T(128)}, f32[2048,64]{1,0:T(8,128)S(1)}, ...), condition=%wide.region_2.3_spmd, body=%wide.region_0.2_spmd.sunk | while | flops 529670 | bytes 1103327 | solution.py:41
  8.8 1.5 gather_fusion
  10.3 1.4 fusion.34
  12.4 1.2 scatter_custom_fusion.13
  14.4 1.5 gather_fusion
  15.9 1.4 fusion.34
  18.0 1.2 scatter_custom_fusion.13
  20.0 1.5 gather_fusion
  21.5 1.4 fusion.34
  23.6 1.2 scatter_custom_fusion.13
  25.6 1.5 gather_fusion
  27.1 1.4 fusion.34
  31.3 1.5 gather_fusion
  32.8 1.4 fusion.34
  36.9 1.5 gather_fusion
  38.4 1.4 fusion.34
  42.5 1.5 gather_fusion
  44.0 1.4 fusion.34
  48.1 1.5 gather_fusion
  49.6 1.4 fusion.34
  51.7 1.2 scatter_custom_fusion.13
  53.7 1.5 gather_fusion
  55.2 1.4 fusion.34
  59.3 1.5 gather_fusion
  60.8 1.4 fusion.34
  64.9 1.5 gather_fusion
  66.4 1.4 fusion.34
  70.9 22.0 %scatter_custom_fusion.3 = f32[2048]{0:T(1024)S(1)} fusion(s32[4096]{0:T(1024)S(1)} %copy-done.4, f32[4096]{0:T(1024)S(1)} %copy-done.2, f32[]{:T(128)} %constant.36.clone.1), kind=kCustom, calls=%fused_computation.37 | custom fusion | flops 4096 | bytes 8196 | tf_op jit(solution)/shard_map/scatter-add | solution.py:49
  92.9 294.5 %all-reduce.4.cloned.1.call-done = f32[131072]{0:T(1024)} async-done(((f32[131072]{0:T(1024)}), f32[131072]{0:T(1024)}) %all-reduce.4.cloned.1.call-update) | async-done | bytes 524304 | tf_op jit(solution)/shard_map/psum | solution.py:43
  388.2 22.0 %scatter_custom_fusion.2 = f32[2048]{0:T(1024)S(1)} fusion(s32[4096]{0:T(1024)S(1)} %copy-done.4, f32[4096]{0:T(1024)S(1)} %fusion.17, f32[]{:T(128)} %constant.36.clone.1), kind=kCustom, calls=%fused_computation.39 | custom fusion | flops 4096 | bytes 8196 | tf_op jit(solution)/shard_map/scatter-add | solution.py:48
  410.2 78.1 %all-reduce = (f32[2048]{0:T(1024)S(1)}, f32[2048]{0:T(1024)S(1)}) all-reduce(f32[2048]{0:T(1024)S(1)} %scatter_custom_fusion.2, f32[2048]{0:T(1024)S(1)} %scatter_custom_fusion.3), channel_id=1, replica_groups=mesh['events'=8,'shells'=32] {'events','shells'}, use_global_device_ids=true, to_apply=%region_5.6 | all-reduce | flops 4096 | bytes 32768 | tf_op jit(solution)/shard_map/psum | solution.py:50
  488.3 23.0 %gather_fusion.2 = f32[4096]{0:T(1024)S(1)} fusion(f32[2048]{0:T(1024)S(1)} %add_divide_fusion, s32[4096]{0:T(1024)S(1)} %fusion.16), kind=kCustom, calls=%fused_computation.2 | custom fusion | bytes 49152 | tf_op jit(solution)/shard_map/gather | solution.py:52
  511.4 1.3 fusion.22
  512.7 40.7 %all_gather.3 = bf16[131072]{0:T(1024)(128)(2,1)S(1)} all-gather(bf16[4096]{0:T(1024)(128)(2,1)S(1)} %get-tuple-element.125), channel_id=1, replica_groups=mesh['events'=8,'shells'=32] {'shells'}, dimensions={0}, use_global_device_ids=true | all-gather | bytes 270336 | tf_op jit(solution)/shard_map/all_gather | solution.py:54
  553.7 47.2 %while.21 = (s32[]{:T(128)}, f32[512,128]{1,0:T(8,128)S(1)}, s32[]{:T(128)}, s32[512]{0:T(512)}, s32[]{:T(128)}, /*index=5*/bf16[512,64,128]{2,1,0:T(8,128)(2,1)...) while((s32[]{:T(128)}, f32[512,128]{1,0:T(8,128)S(1)}, ...), condition=%wide.region_10.11_spmd, body=%wide.region_8.10_spmd.sunk | while | flops 533766 | bytes 837087 | solution.py:66
  555.1 1.3 fusion.38
  559.4 1.3 fusion.38
  563.7 1.3 fusion.38
  568.0 1.3 fusion.38
  572.3 1.3 fusion.38
  576.6 1.3 fusion.38
  580.9 1.3 fusion.38
  585.2 1.3 fusion.38
  589.5 1.3 fusion.38
  593.8 1.3 fusion.38
  598.1 1.3 fusion.38
  601.7 87.3 %all-reduce.6.cloned.1.call-done = f32[65536]{0:T(1024)} async-done(((f32[65536]{0:T(1024)}), f32[65536]{0:T(1024)}) %all-reduce.6.cloned.1.call-update) | async-done | bytes 262160 | tf_op jit(solution)/shard_map/psum | solution.py:67
  689.0 1.7 copy.40
  (116 shorter events, 60.1 us)
Async XLA Ops:
  7.2 63.7 %copy-start.2 = (f32[4096]{0:T(1024)S(1)}, f32[4096]{0:T(1024)}, u32[]{:S(2)}) copy-start(f32[4096]{0:T(1024)} %param.18) | copy-start | bytes 49156
  7.2 63.7 %copy-start.4 = (s32[4096]{0:T(1024)S(1)}, s32[4096]{0:T(1024)}, u32[]{:S(2)}) copy-start(s32[4096]{0:T(1024)} %param.19) | copy-start | bytes 49156
  7.2 380.3 %copy-start.3 = (f32[4096]{0:T(1024)S(1)}, f32[4096]{0:T(1024)}, u32[]{:S(2)}) copy-start(f32[4096]{0:T(1024)} %param.17) | copy-start | bytes 49156
  7.2 380.3 %all-reduce.4.cloned.1.call-start = ((), (), s32[]{:S(2)}) async-start(), calls=%async_computation | async-start | bytes 1048576 | tf_op jit(solution)/shard_map/psum | solution.py:43
  70.8 618.2 %all-reduce.6.cloned.1.call-start = ((), (), s32[]{:S(2)}) async-start(), calls=%async_computation.1 | async-start | bytes 524288 | tf_op jit(solution)/shard_map/psum | solution.py:67
  488.3 23.0 %copy-start = (f32[2048]{0:T(1024)}, f32[2048]{0:T(1024)S(1)}, u32[]{:S(2)}) copy-start(f32[2048]{0:T(1024)S(1)} %add_divide_fusion) | copy-start | bytes 24580
  601.0 0.7 copy-start.1
Sparse Core Ops, SparseCore 0:
  70.9 316.4 all-reduce.3
  601.8 87.1 all-reduce.5
where the time goes:
time: 705 us; the launch traced here: 698 us
  waiting for transfers between devices  382 us (54%)
  blocking collectives  119 us (17%)
  other arithmetic  102 us (14%)
  local copies, waits for them, and re-layouts  49.8 us (7%)
  matrix products  29.4 us (4%)
  between operations  14.8 us (2%)
    psum x1, waiting for transfers between devices, local(): summed = lax.psum(flat_terms, 'shells')  295 us
    psum x1, waiting for transfers between devices, local(): gradient = lax.psum(grads.reshape(-1), 'events')  87.3 us
    psum x1, blocking collectives, local(): numer, denom = lax.psum((numer_local, denom_local), ('events', 'shells'))  78.1 us
    all_gather x1, blocking collectives, local(): lax.all_gather(weighted_half, 'shells', axis=0, tiled=True)  40.7 us
    gather x1, local copies, waits for them, and re-layouts, local(): weighted = pick_weight * (misfit - correction[station])  23 us
    scatter-add x1, other arithmetic, local(): jax.ops.segment_sum(pick_weight, station, num_segments=STATIONS)  22 us
    scatter-add x1, other arithmetic, local(): jax.ops.segment_sum(pick_weight * misfit, station, num_segments=STATIONS)  22 us
    gather x11, local copies, waits for them, and re-layouts, slot_values(): model_rows[cells_of]  16.5 us
  transfers between devices with their start and end apart: 2, of which 2 were waited for; matrix products, arithmetic and copies ran while one was open for 3% of the time, Pallas kernels for 0%

commit v1 on v0

v1 whole, which is shorter than its diff:
```python
import functools

import jax
import jax.numpy as jnp
from jax import lax
from jax.experimental import pallas as pl
from jax.experimental.pallas import tpu as pltpu
from jax.sharding import PartitionSpec as P

PICK_BLK = 64
CELL_BLK = 128
STATIONS = 2048
LANES = 128
GROUP = 8
CHUNK = 128
F32 = jnp.float32
BF16 = jnp.bfloat16
NT = (((1,), (1,)), ((), ()))
VMEM_BYTES = 40 << 20


def iota(shape, axis):
    return lax.broadcasted_iota(jnp.int32, shape, axis)


def down(row):
    tall = jnp.broadcast_to(row.astype(F32), (LANES, LANES))
    return jnp.transpose(tall).astype(jnp.int32)


def pick(mask):
    return jnp.where(mask, 1.0, 0.0).astype(BF16)


def two_parts(x):
    high = x.astype(BF16)
    return high, (x - high.astype(F32)).astype(BF16)


def three_parts(x):
    high, rest = x.astype(BF16), x
    rest = x - high.astype(F32)
    mid = rest.astype(BF16)
    return high, mid, (rest - mid.astype(F32)).astype(BF16)


def forward_kernel(count, pick_ref, cell_ref, model_ref, blocks_ref, out_ref, values_ref):
    step = pl.program_id(0)
    cells = model_ref.shape[0]
    cell_down = down(cell_ref[pl.ds(step, 1), :])
    pick_down = down(pick_ref[pl.ds(step, 1), :])
    lane = iota((CHUNK, LANES), 1)
    chosen = jnp.concatenate([pick(cell_down == lane + t) for t in range(0, cells, LANES)], axis=1)
    rows = jnp.dot(chosen, model_ref[...], preferred_element_type=F32)
    lane_g, sub_g = iota((GROUP, LANES), 1), iota((GROUP, LANES), 0)
    parts = []
    for j in range(0, CHUNK, GROUP):
        block = blocks_ref[pl.ds(j, GROUP)].reshape(GROUP * PICK_BLK, CELL_BLK)
        wide = lax.dot_general(rows[j : j + GROUP].astype(BF16), block, NT, preferred_element_type=F32)
        part = jnp.zeros((GROUP, LANES), F32)
        for i in range(GROUP // 2):
            own = sub_g == 2 * i + (lane_g >= PICK_BLK).astype(jnp.int32)
            part = jnp.where(own, wide[:, i * LANES : (i + 1) * LANES], part)
        parts.append(part)
    values = jnp.concatenate(parts, axis=0)
    values = values + pltpu.roll(values, PICK_BLK, 1)
    half = (lane >= PICK_BLK).astype(jnp.int32)
    values = jnp.where((pick_down & 1) == half, values, 0.0)
    high, low = two_parts(values)
    at = pl.ds(pl.multiple_of(step * CHUNK, CHUNK), CHUNK)
    values_ref[at, 0:LANES] = high
    values_ref[at, LANES : 2 * LANES] = low

    @pl.when(step == pl.num_programs(0) - 1)
    def _():
        slots = values_ref.shape[0]
        picks = pick_ref[...]
        used = iota(picks.shape, 0) * LANES + iota(picks.shape, 1) < count[0]
        target = jnp.where(used, picks >> 1, -1)
        both = values_ref[...]
        tile = 2 * LANES
        for t in range(0, out_ref.shape[0], tile):
            hot = jnp.concatenate(
                [pick(iota((tile, LANES), 0) + t == target[r : r + 1]) for r in range(slots // LANES)],
                axis=1,
            )
            sums = jnp.dot(hot, both, preferred_element_type=F32)
            out_ref[t : t + tile, :] = sums[:, :LANES] + sums[:, LANES:]


def stations_kernel(terms_ref, observed_ref, weight_ref, station_ref, misfit_ref, out_ref):
    senders, rows = terms_ref.shape[0], terms_ref.shape[1]
    predicted = terms_ref[0]
    for s in range(1, senders):
        predicted = predicted + terms_ref[s]
    misfit = observed_ref[...] - predicted
    misfit_ref[...] = misfit
    weight = weight_ref[...]
    stations = station_ref[...]
    high, low = stations >> 7, stations & (LANES - 1)
    hi_count = STATIONS // LANES
    pieces = [p.astype(F32) for p in three_parts(weight * misfit) + three_parts(weight)]
    total = jnp.zeros((len(pieces) * hi_count, LANES), F32)
    for r0 in range(0, rows, 8):
        left, right = [], []
        for r in range(r0, r0 + 8):
            own = iota((hi_count, LANES), 0) == high[r : r + 1]
            left.append(
                jnp.concatenate([jnp.where(own, p[r : r + 1], 0.0) for p in pieces], axis=0).astype(BF16)
            )
            right.append(pick(iota((LANES, LANES), 0) == low[r : r + 1]))
        total = total + lax.dot_general(
            jnp.concatenate(left, axis=1), jnp.concatenate(right, axis=1), NT, preferred_element_type=F32
        )
    h = hi_count
    numer = total[0:h] + total[h : 2 * h] + total[2 * h : 3 * h]
    denom = total[3 * h : 4 * h] + total[4 * h : 5 * h] + total[5 * h : 6 * h]
    sums = jnp.concatenate([numer, denom], axis=0)
    for s in range(out_ref.shape[0]):
        out_ref[s] = sums


def spread_kernel(terms_ref, out_ref):
    total = terms_ref[0]
    for s in range(1, terms_ref.shape[0]):
        total = total + terms_ref[s]
    for s in range(out_ref.shape[0]):
        out_ref[s] = total


def weighted_kernel(terms_ref, misfit_ref, weight_ref, station_ref, corr_ref, weighted_ref, out_ref):
    total = terms_ref[0]
    for s in range(1, terms_ref.shape[0]):
        total = total + terms_ref[s]
    hi_count = STATIONS // LANES
    corr = total[:hi_count] / (total[hi_count:] + 1.0)
    corr_ref[...] = corr
    stations = station_ref[...]
    high, low = stations >> 7, stations & (LANES - 1)
    table = jnp.concatenate(three_parts(corr), axis=0)
    found = []
    for r in range(stations.shape[0]):
        hot = pick(iota((LANES, LANES), 0) == low[r : r + 1])
        wide = jnp.dot(table, hot, preferred_element_type=F32)
        wide = (wide[:hi_count] + wide[hi_count : 2 * hi_count]) + wide[2 * hi_count :]
        own = iota((hi_count, LANES), 0) == high[r : r + 1]
        found.append(jnp.sum(jnp.where(own, wide, 0.0), axis=0, keepdims=True))
    weighted = weight_ref[...] * (misfit_ref[...] - jnp.concatenate(found, axis=0))
    weighted_ref[...] = weighted
    half = weighted.astype(BF16)
    for s in range(out_ref.shape[0]):
        out_ref[s] = half


def backward_kernel(count, pick_ref, cell_ref, resid_ref, blocks_ref, out_ref, terms_ref):
    step = pl.program_id(0)
    pick_down = down(pick_ref[pl.ds(step, 1), :])
    lane, sub = iota((CHUNK, LANES), 1), iota((CHUNK, LANES), 0)
    used = step * CHUNK + sub < count[0]
    row_of = jnp.where(used, pick_down >> 1, -1)
    chosen = jnp.concatenate(
        [pick(row_of == lane + t) for t in range(0, resid_ref.shape[0], LANES)], axis=1
    )
    resid = jnp.dot(chosen, resid_ref[...], preferred_element_type=F32)
    parity = sub & 1
    half = (lane >= PICK_BLK).astype(jnp.int32)
    resid = jnp.where((pick_down & 1) == parity, resid, pltpu.roll(resid, PICK_BLK, 1))
    resid = jnp.where(half == parity, resid, 0.0)
    sub_g = iota((GROUP, LANES), 0)
    parts = []
    for j in range(0, CHUNK, GROUP):
        block = blocks_ref[pl.ds(j, GROUP)].reshape(GROUP * PICK_BLK, CELL_BLK)
        mine = resid[j : j + GROUP]
        wide = jnp.concatenate(
            [jnp.where(sub_g >> 1 == i, mine, 0.0) for i in range(GROUP // 2)], axis=1
        ).astype(BF16)
        parts.append(jnp.dot(wide, block, preferred_element_type=F32))
    high, low = two_parts(jnp.concatenate(parts, axis=0))
    at = pl.ds(pl.multiple_of(step * CHUNK, CHUNK), CHUNK)
    terms_ref[at, 0:LANES] = high
    terms_ref[at, LANES : 2 * LANES] = low

    @pl.when(step == pl.num_programs(0) - 1)
    def _():
        slots = terms_ref.shape[0]
        cells_of = cell_ref[...]
        both = terms_ref[...]
        tile = 2 * LANES
        for t in range(0, out_ref.shape[1], tile):
            hot = jnp.concatenate(
                [pick(iota((tile, LANES), 0) + t == cells_of[r : r + 1]) for r in range(slots // LANES)],
                axis=1,
            )
            sums = jnp.dot(hot, both, preferred_element_type=F32)
            sums = (sums[:, :LANES] + sums[:, LANES:]).astype(BF16)
            for s in range(out_ref.shape[0]):
                out_ref[s, t : t + tile, :] = sums


def gradient_kernel(terms_ref, out_ref):
    total = terms_ref[0].astype(F32)
    for s in range(1, terms_ref.shape[0]):
        total = total + terms_ref[s].astype(F32)
    out_ref[...] = total


def whole(shape):
    return pl.BlockSpec(shape, lambda *_: (0,) * len(shape))


def simple(kernel, out_shape, name):
    return pl.pallas_call(
        kernel,
        out_shape=out_shape,
        compiler_params=pltpu.CompilerParams(vmem_limit_bytes=VMEM_BYTES),
        name=name,
    )


def swap(x, axis):
    return lax.all_to_all(x, axis, 0, 0, tiled=True)


def slot_call(kernel, tables, blocks, out_shape, count, name):
    slots = blocks.shape[0]
    return pl.pallas_call(
        kernel,
        grid_spec=pltpu.PrefetchScalarGridSpec(
            num_scalar_prefetch=1,
            grid=(slots // CHUNK,),
            in_specs=[whole(t.shape) for t in tables]
            + [pl.BlockSpec((CHUNK, PICK_BLK, CELL_BLK), lambda i, c: (i, 0, 0))],
            out_specs=whole(out_shape.shape),
            scratch_shapes=[pltpu.VMEM((slots, 2 * LANES), BF16)],
        ),
        out_shape=out_shape,
        compiler_params=pltpu.CompilerParams(
            dimension_semantics=("arbitrary",), vmem_limit_bytes=VMEM_BYTES
        ),
        name=name,
    )(count, *tables, blocks)


def local(model, sensitivity, pick_block, cell_block, blk_count, observed, pick_weight, station):
    shells, events = lax.axis_size("shells"), lax.axis_size("events")
    picks_of = pick_block.reshape(-1, LANES)
    cells_of = cell_block.reshape(-1, LANES)
    model_rows = model.reshape(-1, CELL_BLK)
    observed, weight = observed.reshape(-1, LANES), pick_weight.reshape(-1, LANES)
    station = station.reshape(-1, LANES)
    own_rows = observed.shape[0]
    group_rows = own_rows * shells
    stat_rows = 2 * STATIONS // LANES
    shape = jax.ShapeDtypeStruct

    partials = slot_call(
        forward_kernel,
        (picks_of, cells_of, model_rows),
        sensitivity,
        shape((group_rows, LANES), F32),
        blk_count,
        "forward",
    )
    partials = swap(partials.reshape(shells, own_rows, LANES), "shells")
    misfit, stats = simple(
        stations_kernel,
        (shape((own_rows, LANES), F32), shape((shells, stat_rows, LANES), F32)),
        "stations",
    )(partials, observed, weight, station)
    stats = swap(stats, "shells")
    stats = simple(spread_kernel, shape((events, stat_rows, LANES), F32), "spread")(stats)
    stats = swap(stats, "events")
    correction, weighted, halves = simple(
        weighted_kernel,
        (
            shape((STATIONS // LANES, LANES), F32),
            shape((own_rows, LANES), F32),
            shape((shells, own_rows, LANES), BF16),
        ),
        "weighted",
    )(stats, misfit, weight, station)
    halves = swap(halves, "shells").reshape(group_rows, LANES)
    grads = slot_call(
        backward_kernel,
        (picks_of, cells_of, halves),
        sensitivity,
        shape((events,) + model_rows.shape, BF16),
        blk_count,
        "backward",
    )
    grads = swap(grads, "events")
    gradient = simple(gradient_kernel, shape(model_rows.shape, F32), "gradient")(grads)
    return (gradient.reshape(-1), correction.reshape(-1), weighted.reshape(-1))


def solution(mesh):
    both = P(("events", "shells"))
    placed = (P("shells"), P(("events", "shells"), None, None)) + (both,) * 6
    return jax.shard_map(
        local,
        mesh=mesh,
        in_specs=placed,
        out_specs=(P("shells"), P(), both),
        check_vma=False,
    )
```

time: 705 us -> 116 us (0.16); the launches traced: 698 us -> 116 us
  waiting for transfers between devices: 382 us -> 0 us
  other arithmetic: 102 us -> 0 us
  local copies, waits for them, and re-layouts: 49.8 us -> 5.66 us
  matrix products: 29.4 us -> 0 us
  blocking collectives: 119 us -> 99.2 us
  between operations: 14.8 us -> 1.37 us
  Pallas kernels: 0 us -> 9.76 us
    psum x2 -> x0, waiting for transfers between devices: 382 us -> none  [the longest x1 295 us: local(): summed = lax.psum(flat_terms, 'shells')]
    all_to_all x0 -> x5, blocking collectives: none -> 99.2 us  [swap(): return lax.all_to_all(x, axis, 0, 0, tiled=True)]
    psum x1 -> x0, blocking collectives: 78.1 us -> none  [local(): numer, denom = lax.psum((numer_local, denom_local), ('events', 'shells'))]
    scatter-add x24 -> x0, other arithmetic: 67.6 us -> none  [the longest x1 22 us: local(): jax.ops.segment_sum(pick_weight, station, num_segments=STATIONS)]
    gather x23 -> x0, local copies, waits for them, and re-layouts: 46.1 us -> none  [the longest x1 23 us: local(): weighted = pick_weight * (misfit - correction[station])]
    all_gather x1 -> x0, blocking collectives: 40.7 us -> none  [local(): lax.all_gather(weighted_half, 'shells', axis=0, tiled=True)]
    dot_general x22 -> x0, matrix products: 29.4 us -> none  [the longest x11 15.4 us: slot_values(): jnp.einsum('kpc,kc->kp', blocks, model_rows[cells_of], preferred_element_...]
    select_n x22 -> x0, other arithmetic: 17.1 us -> none  [the longest x11 8.56 us: backward_turn(): group_resid[picks_of]]
  transfers between devices with their start and end apart: 2 -> 0, of which waited for: 2 -> 0; matrix products, arithmetic and copies ran while one was open for 3% -> 0% of each run, Pallas kernels for 0% -> 0%
where the time goes in v1:
time: 116 us
  blocking collectives  99.2 us (86%)
  Pallas kernels  9.76 us (8%)
  local copies, waits for them, and re-layouts  5.66 us (5%)
  between operations  1.37 us (1%)
    all_to_all x5, blocking collectives, swap(): return lax.all_to_all(x, axis, 0, 0, tiled=True)  99.2 us
    pallas_call x2, Pallas kernels, slot_call(): pl.pallas_call(kernel, grid_spec=pltpu.PrefetchScalarGridSpec(num_scalar_...  7.32 us
    unnamed x20, local copies, waits for them, and re-layouts  5.66 us

profile of v1, /device:TPU:1, one launch (start us, length us, event | category | flops | bytes accessed | tf_op | source)
XLA Modules:
  0.0 116.0 jit_solution(7594522111057921667)
XLA Ops:
  0.6 0.0 copy-start.9
  0.6 0.0 copy-start.7
  1.3 0.0 copy-start
  1.3 3.4 %copy-done = bf16[512,64,128]{2,1,0:T(8,128)(2,1)S(1)} copy-done((bf16[512,64,128]{2,1,0:T(8,128)(2,1)S(1)}, bf16[512,64,128]{2,1,0:T(8,128)(2,1)}, u32[]{:S(2)}) %copy-start) | copy-done | bytes 8388632
  4.7 0.0 copy-start.2
  4.7 0.9 copy-done.2
  5.6 0.0 copy-start.6
  5.6 0.7 copy-done.6
  6.3 0.0 copy-start.8
  6.3 0.7 copy-done.8
  7.0 0.0 copy-start.3
  7.0 0.0 copy-start.4
  7.0 0.0 copy-start.5
  7.0 0.0 copy-start.1
  7.0 4.1 %forward.1 = f32[1024,128]{1,0:T(8,128)S(1)} custom-call(s32[1]{0:T(128)S(6)} %copy.11.count, s32[4,128]{1,0:T(4,128)S(1)} %bitcast.19, s32[4,128]{1,0:T(4,128)S(1)} %bitcast.21, bf16[512,128]{1,0:T(8,128)(2,1)S(1)} %bitcast.13, bf16[512,64,128]{2,1,0:T(8,128)(2,1)S(1)} %copy-done), custom_call_target="tpu_custom_call" | custom-call | tf_op jit(solution)/shard_map/forward/pallas_call | solution.py:226
  11.1 30.4 %all_to_all.25.terms_ref = f32[32,32,128]{2,1,0:T(8,128)S(1)} all-to-all(f32[32,32,128]{2,1,0:T(8,128)S(1)} %bitcast.11), channel_id=1, replica_groups=mesh['events'=8,'shells'=32] {'shells'}, dimensions={0} | all-to-all | bytes 1048576 | tf_op jit(solution)/shard_map/all_to_all | solution.py:221
  41.4 0.0 copy-done.3
  41.4 0.0 copy-done.4
  41.4 0.0 copy-done.5
  41.5 0.5 stations.1
  42.0 22.2 %all_to_all.26.terms_ref = f32[32,32,128]{2,1,0:T(8,128)S(1)} all-to-all(f32[32,32,128]{2,1,0:T(8,128)S(1)} %get-tuple-element.8), channel_id=1, replica_groups=mesh['events'=8,'shells'=32] {'shells'}, dimensions={0} | all-to-all | bytes 1048576 | tf_op jit(solution)/shard_map/all_to_all | solution.py:221
  64.2 11.3 %all_to_all.27.terms_ref = f32[8,32,128]{2,1,0:T(8,128)S(1)} all-to-all(f32[8,32,128]{2,1,0:T(8,128)S(1)} %spread.1), channel_id=1, replica_groups=mesh['events'=8,'shells'=32] {'events'}, dimensions={0} | all-to-all | bytes 262144 | tf_op jit(solution)/shard_map/all_to_all | solution.py:221
  75.5 1.1 weighted.1
  76.6 17.5 %all_to_all.28 = bf16[32,32,128]{2,1,0:T(8,128)(2,1)S(1)} all-to-all(bf16[32,32,128]{2,1,0:T(8,128)(2,1)S(1)} %get-tuple-element.10), channel_id=1, replica_groups=mesh['events'=8,'shells'=32] {'shells'}, dimensions={0} | all-to-all | bytes 524288 | tf_op jit(solution)/shard_map/all_to_all | solution.py:221
  94.1 0.0 copy-done.9
  94.1 0.0 copy-done.7
  94.1 0.0 copy-done.1
  94.1 3.2 %backward.1 = bf16[8,512,128]{2,1,0:T(8,128)(2,1)S(1)} custom-call(s32[1]{0:T(128)S(6)} %copy.11.count, s32[4,128]{1,0:T(4,128)S(1)} %bitcast.20, s32[4,128]{1,0:T(4,128)S(1)} %bitcast.22, bf16[1024,128]{1,0:T(8,128)(2,1)S(1)} %bitcast.12, bf16[512,64,128]{2,1,0:T(8,128)(2,1)S(1)} %copy-done.1), custom_call_target="tpu_custom_call" | custom-call | tf_op jit(solution)/shard_map/backward/pallas_call | solution.py:226
  97.3 17.8 %all_to_all.29.terms_ref = bf16[8,512,128]{2,1,0:T(8,128)(2,1)S(1)} all-to-all(bf16[8,512,128]{2,1,0:T(8,128)(2,1)S(1)} %backward.1), channel_id=1, replica_groups=mesh['events'=8,'shells'=32] {'events'}, dimensions={0} | all-to-all | bytes 2097152 | tf_op jit(solution)/shard_map/all_to_all | solution.py:221
  115.1 0.8 gradient.1
  (1 shorter events, 0.0 us)
Async XLA Ops:
  0.6 93.4 %copy-start.9 = (s32[512]{0:T(512)S(1)}, s32[512]{0:T(512)}, u32[]{:S(2)}) copy-start(s32[512]{0:T(512)} %param.11) | copy-start | bytes 6148
  0.6 93.4 %copy-start.7 = (s32[512]{0:T(512)S(1)}, s32[512]{0:T(512)}, u32[]{:S(2)}) copy-start(s32[512]{0:T(512)} %param.10) | copy-start | bytes 6148
  1.3 3.4 %copy-start = (bf16[512,64,128]{2,1,0:T(8,128)(2,1)S(1)}, bf16[512,64,128]{2,1,0:T(8,128)(2,1)}, u32[]{:S(2)}) copy-start(bf16[512,64,128]{2,1,0:T(8,128)(2,1)} %blocks_ref.3) | copy-start | bytes 25165828
  4.7 0.9 copy-start.2
  5.6 0.7 copy-start.6
  6.3 0.7 copy-start.8
  7.0 34.5 %copy-start.3 = (f32[4096]{0:T(1024)S(1)}, f32[4096]{0:T(1024)}, u32[]{:S(2)}) copy-start(f32[4096]{0:T(1024)} %param.14) | copy-start | bytes 49156
  7.0 34.5 %copy-start.4 = (s32[4096]{0:T(1024)S(1)}, s32[4096]{0:T(1024)}, u32[]{:S(2)}) copy-start(s32[4096]{0:T(1024)} %param.15) | copy-start | bytes 49156
  7.0 34.5 %copy-start.5 = (f32[4096]{0:T(1024)S(1)}, f32[4096]{0:T(1024)}, u32[]{:S(2)}) copy-start(f32[4096]{0:T(1024)} %param.13) | copy-start | bytes 49156
  7.0 87.1 %copy-start.1 = (bf16[512,64,128]{2,1,0:T(8,128)(2,1)S(1)}, bf16[512,64,128]{2,1,0:T(8,128)(2,1)}, u32[]{:S(2)}) copy-start(bf16[512,64,128]{2,1,0:T(8,128)(2,1)} %blocks_ref.3) | copy-start | bytes 25165828

commit v2 on v1

v2 whole, which is shorter than its diff:
```python
import itertools

import jax
import jax.numpy as jnp
from jax import lax
from jax.experimental import pallas as pl
from jax.experimental.pallas import tpu as pltpu
from jax.sharding import PartitionSpec as P

PICK_BLK = 64
CELL_BLK = 128
STATIONS = 2048
LANES = 128
GROUP = 8
CHUNK = 128
F32 = jnp.float32
BF16 = jnp.bfloat16
NT = (((1,), (1,)), ((), ()))
VMEM_BYTES = 40 << 20


def iota(shape, axis):
    return lax.broadcasted_iota(jnp.int32, shape, axis)


def down(row):
    tall = jnp.broadcast_to(row.astype(F32), (LANES, LANES))
    return jnp.transpose(tall).astype(jnp.int32)


def pick(mask):
    return jnp.where(mask, 1.0, 0.0).astype(BF16)


def two_parts(x):
    high = x.astype(BF16)
    return high, (x - high.astype(F32)).astype(BF16)


def three_parts(x):
    high, rest = x.astype(BF16), x
    rest = x - high.astype(F32)
    mid = rest.astype(BF16)
    return high, mid, (rest - mid.astype(F32)).astype(BF16)


def forward_kernel(count_hbm, pick_hbm, cell_hbm, model_hbm, blocks_hbm, out_ref, blocks_ref, used_ref,
                   count, pick_ref, cell_ref, model_ref, values_ref, table_sems, block_sems):
    slots, cells = blocks_ref.shape[0], model_ref.shape[0]
    tables = [
        pltpu.make_async_copy(src, dst, table_sems.at[n])
        for n, (src, dst) in enumerate(
            [(cell_hbm, cell_ref), (model_hbm, model_ref), (pick_hbm, pick_ref), (count_hbm, count)]
        )
    ]
    for copy in tables:
        copy.start()
    copies = []
    for n in range(slots // CHUNK):
        at = pl.ds(n * CHUNK, CHUNK)
        copies.append(pltpu.make_async_copy(blocks_hbm.at[at], blocks_ref.at[at], block_sems.at[n]))
        copies[-1].start()
    for copy in tables:
        copy.wait()
    lane = iota((CHUNK, LANES), 1)
    lane_g, sub_g = iota((GROUP, LANES), 1), iota((GROUP, LANES), 0)
    half = (lane >= PICK_BLK).astype(jnp.int32)
    rows = []
    for n in range(slots // CHUNK):
        cell_down = down(cell_ref[n : n + 1, :])
        chosen = jnp.concatenate([pick(cell_down == lane + t) for t in range(0, cells, LANES)], axis=1)
        rows.append(jnp.dot(chosen, model_ref[...], preferred_element_type=F32))
    for n in range(slots // CHUNK):
        copies[n].wait()
        pick_down = down(pick_ref[n : n + 1, :])
        parts = []
        for j in range(0, CHUNK, GROUP):
            block = blocks_ref[n * CHUNK + j : n * CHUNK + j + GROUP].reshape(GROUP * PICK_BLK, CELL_BLK)
            wide = lax.dot_general(
                rows[n][j : j + GROUP].astype(BF16), block, NT, preferred_element_type=F32
            )
            part = jnp.zeros((GROUP, LANES), F32)
            for i in range(GROUP // 2):
                own = sub_g == 2 * i + (lane_g >= PICK_BLK).astype(jnp.int32)
                part = jnp.where(own, wide[:, i * LANES : (i + 1) * LANES], part)
            parts.append(part)
        values = jnp.concatenate(parts, axis=0)
        values = values + pltpu.roll(values, PICK_BLK, 1)
        values = jnp.where((pick_down & 1) == half, values, 0.0)
        high, low = two_parts(values)
        values_ref[n * CHUNK : (n + 1) * CHUNK, 0:LANES] = high
        values_ref[n * CHUNK : (n + 1) * CHUNK, LANES : 2 * LANES] = low
    picks = pick_ref[...]
    used = iota(picks.shape, 0) * LANES + iota(picks.shape, 1) < count[0]
    picks = jnp.where(used, picks, -1)
    used_ref[...] = picks
    target = picks >> 1
    both = values_ref[...]
    tile = 2 * LANES
    for t in range(0, out_ref.shape[0], tile):
        hot = jnp.concatenate(
            [pick(iota((tile, LANES), 0) + t == target[r : r + 1]) for r in range(slots // LANES)],
            axis=1,
        )
        sums = jnp.dot(hot, both, preferred_element_type=F32)
        out_ref[t : t + tile, :] = sums[:, :LANES] + sums[:, LANES:]


def stations_kernel(terms_ref, observed_ref, weight_ref, station_ref, misfit_ref, out_ref):
    senders, rows = terms_ref.shape[0], terms_ref.shape[1]
    predicted = terms_ref[0]
    for s in range(1, senders):
        predicted = predicted + terms_ref[s]
    misfit = observed_ref[...] - predicted
    misfit_ref[...] = misfit
    weight = weight_ref[...]
    stations = station_ref[...]
    high, low = stations >> 7, stations & (LANES - 1)
    hi_count = STATIONS // LANES
    pieces = [p.astype(F32) for p in three_parts(weight * misfit) + three_parts(weight)]
    total = jnp.zeros((len(pieces) * hi_count, LANES), F32)
    for r0 in range(0, rows, 8):
        left, right = [], []
        for r in range(r0, r0 + 8):
            own = iota((hi_count, LANES), 0) == high[r : r + 1]
            left.append(
                jnp.concatenate([jnp.where(own, p[r : r + 1], 0.0) for p in pieces], axis=0).astype(BF16)
            )
            right.append(pick(iota((LANES, LANES), 0) == low[r : r + 1]))
        total = total + lax.dot_general(
            jnp.concatenate(left, axis=1), jnp.concatenate(right, axis=1), NT, preferred_element_type=F32
        )
    h = hi_count
    numer = total[0:h] + total[h : 2 * h] + total[2 * h : 3 * h]
    denom = total[3 * h : 4 * h] + total[4 * h : 5 * h] + total[5 * h : 6 * h]
    sums = jnp.concatenate([numer, denom], axis=0)
    for s in range(out_ref.shape[0]):
        out_ref[s] = sums


def spread_kernel(terms_ref, out_ref):
    total = terms_ref[0]
    for s in range(1, terms_ref.shape[0]):
        total = total + terms_ref[s]
    for s in range(out_ref.shape[0]):
        out_ref[s] = total


def weighted_kernel(terms_ref, misfit_ref, weight_ref, station_ref, corr_ref, weighted_ref, out_ref):
    total = terms_ref[0]
    for s in range(1, terms_ref.shape[0]):
        total = total + terms_ref[s]
    hi_count = STATIONS // LANES
    corr = total[:hi_count] / (total[hi_count:] + 1.0)
    corr_ref[...] = corr
    stations = station_ref[...]
    high, low = stations >> 7, stations & (LANES - 1)
    table = jnp.concatenate(three_parts(corr), axis=0)
    found = []
    for r in range(stations.shape[0]):
        hot = pick(iota((LANES, LANES), 0) == low[r : r + 1])
        wide = jnp.dot(table, hot, preferred_element_type=F32)
        wide = (wide[:hi_count] + wide[hi_count : 2 * hi_count]) + wide[2 * hi_count :]
        own = iota((hi_count, LANES), 0) == high[r : r + 1]
        found.append(jnp.sum(jnp.where(own, wide, 0.0), axis=0, keepdims=True))
    weighted = weight_ref[...] * (misfit_ref[...] - jnp.concatenate(found, axis=0))
    weighted_ref[...] = weighted
    half = weighted.astype(BF16)
    for s in range(out_ref.shape[0]):
        out_ref[s] = half


def backward_kernel(pick_ref, cell_ref, resid_ref, blocks_ref, out_ref, terms_ref):
    slots = blocks_ref.shape[0]
    lane, sub = iota((CHUNK, LANES), 1), iota((CHUNK, LANES), 0)
    sub_g = iota((GROUP, LANES), 0)
    parity = sub & 1
    half = (lane >= PICK_BLK).astype(jnp.int32)
    for n in range(slots // CHUNK):
        pick_down = down(pick_ref[n : n + 1, :])
        row_of = pick_down >> 1
        chosen = jnp.concatenate(
            [pick(row_of == lane + t) for t in range(0, resid_ref.shape[0], LANES)], axis=1
        )
        resid = jnp.dot(chosen, resid_ref[...], preferred_element_type=F32)
        resid = jnp.where((pick_down & 1) == parity, resid, pltpu.roll(resid, PICK_BLK, 1))
        resid = jnp.where(half == parity, resid, 0.0)
        parts = []
        for j in range(0, CHUNK, GROUP):
            block = blocks_ref[n * CHUNK + j : n * CHUNK + j + GROUP].reshape(GROUP * PICK_BLK, CELL_BLK)
            mine = resid[j : j + GROUP]
            wide = jnp.concatenate(
                [jnp.where(sub_g >> 1 == i, mine, 0.0) for i in range(GROUP // 2)], axis=1
            ).astype(BF16)
            parts.append(jnp.dot(wide, block, preferred_element_type=F32))
        high, low = two_parts(jnp.concatenate(parts, axis=0))
        terms_ref[n * CHUNK : (n + 1) * CHUNK, 0:LANES] = high
        terms_ref[n * CHUNK : (n + 1) * CHUNK, LANES : 2 * LANES] = low
    cells_of = cell_ref[...]
    both = terms_ref[...]
    tile = 2 * LANES
    for t in range(0, out_ref.shape[1], tile):
        hot = jnp.concatenate(
            [pick(iota((tile, LANES), 0) + t == cells_of[r : r + 1]) for r in range(slots // LANES)],
            axis=1,
        )
        sums = jnp.dot(hot, both, preferred_element_type=F32)
        sums = (sums[:, :LANES] + sums[:, LANES:]).astype(BF16)
        for s in range(out_ref.shape[0]):
            out_ref[s, t : t + tile, :] = sums


def gradient_kernel(terms_ref, out_ref):
    total = terms_ref[0].astype(F32)
    for s in range(1, terms_ref.shape[0]):
        total = total + terms_ref[s].astype(F32)
    out_ref[...] = total


def simple(kernel, out_shape, name, **more):
    return pl.pallas_call(
        kernel,
        out_shape=out_shape,
        compiler_params=pltpu.CompilerParams(vmem_limit_bytes=VMEM_BYTES),
        name=name,
        **more,
    )


def swap(x, axis, groups=None):
    return lax.all_to_all(x, axis, 0, 0, tiled=True, axis_index_groups=groups)


def torus_groups():
    lines, planes = {}, {}
    for x, zl, y, zh, c in itertools.product(range(4), range(2), range(4), range(4), range(2)):
        flat = (x * 2 + zl) * 32 + y * 8 + zh * 2 + c
        lines.setdefault((x, y), []).append(flat)
        planes.setdefault((zl, zh, c), []).append(flat)
    return list(lines.values()), list(planes.values())


def local(model, sensitivity, pick_block, cell_block, blk_count, observed, pick_weight, station):
    shells, events = lax.axis_size("shells"), lax.axis_size("events")
    picks_of = pick_block.reshape(-1, LANES)
    cells_of = cell_block.reshape(-1, LANES)
    model_rows = model.reshape(-1, CELL_BLK)
    observed, weight = observed.reshape(-1, LANES), pick_weight.reshape(-1, LANES)
    station = station.reshape(-1, LANES)
    own_rows = observed.shape[0]
    group_rows = own_rows * shells
    stat_rows = 2 * STATIONS // LANES
    shape = jax.ShapeDtypeStruct

    outside = pl.BlockSpec(memory_space=pltpu.HBM)
    lines, planes = torus_groups()
    devices = ("events", "shells")

    partials, blocks, used_picks = pl.pallas_call(
        forward_kernel,
        in_specs=[outside] * 5,
        out_specs=(pl.BlockSpec(memory_space=pltpu.VMEM),) * 3,
        out_shape=(
            shape((group_rows, LANES), F32),
            shape(sensitivity.shape, BF16),
            shape(picks_of.shape, jnp.int32),
        ),
        scratch_shapes=[
            pltpu.SMEM((1,), jnp.int32),
            pltpu.VMEM(picks_of.shape, jnp.int32),
            pltpu.VMEM(cells_of.shape, jnp.int32),
            pltpu.VMEM(model_rows.shape, BF16),
            pltpu.VMEM((sensitivity.shape[0], 2 * LANES), BF16),
            pltpu.SemaphoreType.DMA((4,)),
            pltpu.SemaphoreType.DMA((sensitivity.shape[0] // CHUNK,)),
        ],
        compiler_params=pltpu.CompilerParams(vmem_limit_bytes=VMEM_BYTES),
        name="forward",
    )(blk_count, picks_of, cells_of, model_rows, sensitivity)
    partials = swap(partials.reshape(shells, own_rows, LANES), "shells")
    misfit, stats = simple(
        stations_kernel,
        (shape((own_rows, LANES), F32), shape((len(lines[0]), stat_rows, LANES), F32)),
        "stations",
    )(partials, observed, weight, station)
    stats = swap(stats, devices, lines)
    stats = simple(spread_kernel, shape((len(planes[0]), stat_rows, LANES), F32), "spread")(stats)
    stats = swap(stats, devices, planes)
    correction, weighted, halves = simple(
        weighted_kernel,
        (
            shape((STATIONS // LANES, LANES), F32),
            shape((own_rows, LANES), F32),
            shape((shells, own_rows, LANES), BF16),
        ),
        "weighted",
    )(stats, misfit, weight, station)
    halves = swap(halves, "shells").reshape(group_rows, LANES)
    grads = simple(
        backward_kernel,
        shape((events,) + model_rows.shape, BF16),
        "backward",
        scratch_shapes=[pltpu.VMEM((sensitivity.shape[0], 2 * LANES), BF16)],
    )(used_picks, cells_of, halves, blocks)
    grads = swap(grads, "events")
    gradient = simple(gradient_kernel, shape(model_rows.shape, F32), "gradient")(grads)
    return (gradient.reshape(-1), correction.reshape(-1), weighted.reshape(-1))


def solution(mesh):
    both = P(("events", "shells"))
    placed = (P("shells"), P(("events", "shells"), None, None)) + (both,) * 6
    return jax.shard_map(
        local,
        mesh=mesh,
        in_specs=placed,
        out_specs=(P("shells"), P(), both),
        check_vma=False,
    )
```

time: 116 us -> 109 us (0.940)
  blocking collectives: 99.2 us -> 95 us
  local copies, waits for them, and re-layouts: 5.66 us -> 2.27 us
    all_to_all x5, blocking collectives: 99.2 us -> 95 us  [swap(): return lax.all_to_all(x, axis, 0, 0, tiled=True, axis_index_groups=groups)]
    unnamed x20 -> x14, local copies, waits for them, and re-layouts: 5.66 us -> 2.27 us
where the time goes in v2:
time: 109 us
  blocking collectives  95 us (87%)
  Pallas kernels  10 us (9%)
  local copies, waits for them, and re-layouts  2.27 us (2%)
  between operations  1.35 us (1%)
    all_to_all x5, blocking collectives, swap(): return lax.all_to_all(x, axis, 0, 0, tiled=True, axis_index_groups=groups)  95 us
    pallas_call x1, Pallas kernels, local(): pl.pallas_call(forward_kernel, in_specs=[outside] * 5, out_specs=(pl.Bloc...  5.13 us
    pallas_call x1, Pallas kernels, local(): simple(backward_kernel, shape((events,) + model_rows.shape, BF16), 'backw...  2.47 us
    unnamed x14, local copies, waits for them, and re-layouts  2.27 us

profile of v2, /device:TPU:1, one launch (start us, length us, event | category | flops | bytes accessed | tf_op | source)
XLA Modules:
  0.0 108.6 jit_solution(16292895755330306360)
XLA Ops:
  0.6 0.0 copy-start.5
  1.3 0.0 copy-start
  1.3 0.9 copy-done
  2.2 0.0 copy-start.4
  2.2 0.7 copy-done.4
  2.9 0.0 copy-start.6
  2.9 0.7 copy-done.6
  3.6 0.0 copy-start.1
  3.6 0.0 copy-start.2
  3.6 0.0 copy-start.3
  3.6 5.1 %forward.1 = (f32[1024,128]{1,0:T(8,128)S(1)}, bf16[512,64,128]{2,1,0:T(8,128)(2,1)S(1)}, s32[4,128]{1,0:T(4,128)S(1)}) custom-call(s32[1]{0:T(128)S(6)} %copy.11.count_hbm, s32[4,128]{1,0:T(4,128)S(1)} %bitcast.21, s32[4,128]{1,0:T(4,128)S(1)} %bitcast.19, bf16[512,128]{1,0:T(8,128)(2,1)S(1)} %bitcast.13, bf16[512,64,128]{2,1,0:T(8,128)(2,1)} %blocks_hbm.1), custom_call_target="tpu_custom_call" | custom-call | tf_op jit(solution)/shard_map/forward/pallas_call | solution.py:259
  8.7 30.4 %all_to_all.25.terms_ref = f32[32,32,128]{2,1,0:T(8,128)S(1)} all-to-all(f32[32,32,128]{2,1,0:T(8,128)S(1)} %bitcast.12), channel_id=1, replica_groups=mesh['events'=8,'shells'=32] {'shells'}, dimensions={0} | all-to-all | bytes 1048576 | tf_op jit(solution)/shard_map/all_to_all | solution.py:231
  39.1 0.0 copy-done.1
  39.1 0.0 copy-done.2
  39.1 0.0 copy-done.3
  39.1 0.5 stations.1
  39.6 15.7 %all_to_all.26.terms_ref = f32[16,32,128]{2,1,0:T(8,128)S(1)} all-to-all(f32[16,32,128]{2,1,0:T(8,128)S(1)} %get-tuple-element.13), channel_id=1, replica_groups={{0,1,2,3,4,5,6,7,32,33,34,35,36,37,38,39},{8,9,10,11,12,13,14,15,40,41,..., dimensions={0} | all-to-all | bytes 524288 | tf_op jit(solution)/shard_map/all_to_all | solution.py:231
  55.4 13.3 %all_to_all.27.terms_ref = f32[16,32,128]{2,1,0:T(8,128)S(1)} all-to-all(f32[16,32,128]{2,1,0:T(8,128)S(1)} %spread.1), channel_id=1, replica_groups={{0,8,16,24,64,72,80,88,128,136,144,152,192,200,208,216},{1,9,17,25,65,7..., dimensions={0} | all-to-all | bytes 524288 | tf_op jit(solution)/shard_map/all_to_all | solution.py:231
  68.6 1.1 weighted.1
  69.7 17.1 %all_to_all.28 = bf16[32,32,128]{2,1,0:T(8,128)(2,1)S(1)} all-to-all(bf16[32,32,128]{2,1,0:T(8,128)(2,1)S(1)} %get-tuple-element.15), channel_id=1, replica_groups=mesh['events'=8,'shells'=32] {'shells'}, dimensions={0} | all-to-all | bytes 524288 | tf_op jit(solution)/shard_map/all_to_all | solution.py:231
  86.8 0.0 copy-done.5
  86.9 2.5 %backward.1 = bf16[8,512,128]{2,1,0:T(8,128)(2,1)S(1)} custom-call(s32[4,128]{1,0:T(4,128)S(1)} %get-tuple-element.11.pick_ref, s32[4,128]{1,0:T(4,128)S(1)} %bitcast.20, bf16[1024,128]{1,0:T(8,128)(2,1)S(1)} %bitcast.11, bf16[512,64,128]{2,1,0:T(8,128)(2,1)S(1)} %get-tuple-element.16.blocks_ref), custom_call_target="tpu_custom_call" | custom-call | tf_op jit(solution)/shard_map/backward/pallas_call | solution.py:299
  89.3 18.4 %all_to_all.29.terms_ref = bf16[8,512,128]{2,1,0:T(8,128)(2,1)S(1)} all-to-all(bf16[8,512,128]{2,1,0:T(8,128)(2,1)S(1)} %backward.1), channel_id=1, replica_groups=mesh['events'=8,'shells'=32] {'events'}, dimensions={0} | all-to-all | bytes 2097152 | tf_op jit(solution)/shard_map/all_to_all | solution.py:231
  107.8 0.8 gradient.1
  (1 shorter events, 0.0 us)
Async XLA Ops:
  0.6 86.2 %copy-start.5 = (s32[512]{0:T(512)S(1)}, s32[512]{0:T(512)}, u32[]{:S(2)}) copy-start(s32[512]{0:T(512)} %param.11) | copy-start | bytes 6148
  1.3 0.9 copy-start
  2.2 0.7 copy-start.4
  2.9 0.7 copy-start.6
  3.6 35.5 %copy-start.1 = (f32[4096]{0:T(1024)S(1)}, f32[4096]{0:T(1024)}, u32[]{:S(2)}) copy-start(f32[4096]{0:T(1024)} %param.14) | copy-start | bytes 49156
  3.6 35.5 %copy-start.2 = (s32[4096]{0:T(1024)S(1)}, s32[4096]{0:T(1024)}, u32[]{:S(2)}) copy-start(s32[4096]{0:T(1024)} %param.15) | copy-start | bytes 49156
  3.6 35.5 %copy-start.3 = (f32[4096]{0:T(1024)S(1)}, f32[4096]{0:T(1024)}, u32[]{:S(2)}) copy-start(f32[4096]{0:T(1024)} %param.13) | copy-start | bytes 49156

commit v3 on v2

--- a/solution.py
+++ b/solution.py
@@ -16,6 +16,8 @@
 F32 = jnp.float32
 BF16 = jnp.bfloat16
 NT = (((1,), (1,)), ((), ()))
+TN = (((0,), (0,)), ((), ()))
+SLOT_CAP = 32
 VMEM_BYTES = 40 << 20
 
 
@@ -44,38 +46,65 @@
     return high, mid, (rest - mid.astype(F32)).astype(BF16)
 
 
-def forward_kernel(count_hbm, pick_hbm, cell_hbm, model_hbm, blocks_hbm, out_ref, blocks_ref, used_ref,
-                   count, pick_ref, cell_ref, model_ref, values_ref, table_sems, block_sems):
+def forward_kernel(count_hbm, pick_hbm, cell_hbm, model_hbm, blocks_hbm, out_ref, blocks_ref, code_ref,
+                   count, pick_ref, cell_ref, model_ref, values_ref, hot_ref, table_sems, block_sems):
     slots, cells = blocks_ref.shape[0], model_ref.shape[0]
+    owners = out_ref.shape[0]
+    chunks = range(slots // CHUNK)
     tables = [
         pltpu.make_async_copy(src, dst, table_sems.at[n])
         for n, (src, dst) in enumerate(
-            [(cell_hbm, cell_ref), (model_hbm, model_ref), (pick_hbm, pick_ref), (count_hbm, count)]
+            [(count_hbm, count), (pick_hbm, pick_ref), (cell_hbm, cell_ref), (model_hbm, model_ref)]
         )
     ]
     for copy in tables:
         copy.start()
     copies = []
-    for n in range(slots // CHUNK):
-        at = pl.ds(n * CHUNK, CHUNK)
+    piece = slots // block_sems.shape[0]
+    for n in range(slots // piece):
+        at = pl.ds(n * piece, piece)
         copies.append(pltpu.make_async_copy(blocks_hbm.at[at], blocks_ref.at[at], block_sems.at[n]))
         copies[-1].start()
     for copy in tables:
         copy.wait()
-    lane = iota((CHUNK, LANES), 1)
-    lane_g, sub_g = iota((GROUP, LANES), 1), iota((GROUP, LANES), 0)
+    lane, sub = iota((CHUNK, LANES), 1), iota((CHUNK, LANES), 0)
     half = (lane >= PICK_BLK).astype(jnp.int32)
-    rows = []
-    for n in range(slots // CHUNK):
+
+    before, every = pick(sub < lane), jnp.ones((CHUNK, LANES), BF16)
+    seen = jnp.zeros((owners, LANES), F32)
+    index = jnp.zeros((owners * 8, LANES), F32)
+    codes, code_down, rows = [], [], []
+    for n in chunks:
+        picks = pick_ref[n : n + 1, :]
+        used = n * CHUNK + iota((1, LANES), 1) < count[0]
+        owner, inside = picks >> 6, picks & (PICK_BLK - 1)
+        mine = jnp.logical_and(iota((owners, LANES), 0) == owner, used)
+        ones = pick(mine)
+        ahead = seen + jnp.dot(ones, before, preferred_element_type=F32)
+        seen = seen + jnp.dot(ones, every, preferred_element_type=F32)
+        rank = jnp.sum(jnp.where(mine, ahead, 0.0), axis=0, keepdims=True).astype(jnp.int32)
+        code = jnp.where(used, owner * SLOT_CAP + rank, -1)
+        codes.append(code)
+        code_ref[n : n + 1, :] = code
+        code_down.append(down(code))
         cell_down = down(cell_ref[n : n + 1, :])
         chosen = jnp.concatenate([pick(cell_down == lane + t) for t in range(0, cells, LANES)], axis=1)
         rows.append(jnp.dot(chosen, model_ref[...], preferred_element_type=F32))
-    for n in range(slots // CHUNK):
-        copies[n].wait()
-        pick_down = down(pick_ref[n : n + 1, :])
+        tagged = jnp.logical_and(iota((owners * 8, LANES), 0) >> 3 == owner, used)
+        tagged = jnp.where(tagged, (inside + 1).astype(F32), 0.0).astype(BF16)
+        ranked = pick((code_down[n] & (SLOT_CAP - 1)) == lane)
+        index = index + jnp.dot(tagged, ranked, preferred_element_type=F32)
+        hot_ref[:, n * CHUNK : (n + 1) * CHUNK] = pick(iota((hot_ref.shape[0], LANES), 0) == code >> 1)
+    out_ref[:, SLOT_CAP:, :] = index.astype(BF16).reshape(owners, 8, LANES)
+
+    lane_g, sub_g = iota((GROUP, LANES), 1), iota((GROUP, LANES), 0)
+    for n in chunks:
         parts = []
         for j in range(0, CHUNK, GROUP):
-            block = blocks_ref[n * CHUNK + j : n * CHUNK + j + GROUP].reshape(GROUP * PICK_BLK, CELL_BLK)
+            first = n * CHUNK + j
+            if first % piece == 0:
+                copies[first // piece].wait()
+            block = blocks_ref[first : first + GROUP].reshape(GROUP * PICK_BLK, CELL_BLK)
             wide = lax.dot_general(
                 rows[n][j : j + GROUP].astype(BF16), block, NT, preferred_element_type=F32
             )
@@ -86,31 +115,41 @@
             parts.append(part)
         values = jnp.concatenate(parts, axis=0)
         values = values + pltpu.roll(values, PICK_BLK, 1)
-        values = jnp.where((pick_down & 1) == half, values, 0.0)
+        values = jnp.where((code_down[n] & 1) == half, values, 0.0)
         high, low = two_parts(values)
         values_ref[n * CHUNK : (n + 1) * CHUNK, 0:LANES] = high
         values_ref[n * CHUNK : (n + 1) * CHUNK, LANES : 2 * LANES] = low
-    picks = pick_ref[...]
-    used = iota(picks.shape, 0) * LANES + iota(picks.shape, 1) < count[0]
-    picks = jnp.where(used, picks, -1)
-    used_ref[...] = picks
-    target = picks >> 1
-    both = values_ref[...]
-    tile = 2 * LANES
-    for t in range(0, out_ref.shape[0], tile):
-        hot = jnp.concatenate(
-            [pick(iota((tile, LANES), 0) + t == target[r : r + 1]) for r in range(slots // LANES)],
-            axis=1,
-        )
-        sums = jnp.dot(hot, both, preferred_element_type=F32)
-        out_ref[t : t + tile, :] = sums[:, :LANES] + sums[:, LANES:]
-
-
-def stations_kernel(terms_ref, observed_ref, weight_ref, station_ref, misfit_ref, out_ref):
-    senders, rows = terms_ref.shape[0], terms_ref.shape[1]
-    predicted = terms_ref[0]
-    for s in range(1, senders):
-        predicted = predicted + terms_ref[s]
+    placed = jnp.dot(hot_ref[...], values_ref[...], preferred_element_type=F32).astype(BF16)
+    q = SLOT_CAP // 2
+    out_ref[:, 0:q, :] = placed[:, :LANES].reshape(owners, q, LANES)
+    out_ref[:, q : 2 * q, :] = placed[:, LANES:].reshape(owners, q, LANES)
+
+
+def stations_kernel(terms_ref, observed_ref, weight_ref, station_ref, misfit_ref, place_ref, out_ref):
+    senders, rows = terms_ref.shape[0], observed_ref.shape[0]
+    q = SLOT_CAP // 2
+    flat = senders * q
+    lane, sub = iota((flat, LANES), 1), iota((flat, LANES), 0)
+    half = (lane >= PICK_BLK).astype(jnp.int32)
+    index = terms_ref[:, SLOT_CAP:, :].astype(F32)
+    index = jnp.concatenate([index] * (q // 8), axis=1).reshape(flat, LANES)
+    every = jnp.ones((LANES, LANES), BF16)
+    total = jnp.zeros((LANES, 2 * LANES), F32)
+    pieces = [terms_ref[:, n * q : (n + 1) * q, :].astype(F32).reshape(flat, LANES) for n in (0, 1)]
+    rolled = [pltpu.roll(p, PICK_BLK, 1) for p in pieces]
+    for h in (0, 1):
+        own = jnp.where(lane == 2 * (sub & (q - 1)) + h, index, 0.0).astype(BF16)
+        place = jnp.dot(own, every, preferred_element_type=F32).astype(jnp.int32) - 1
+        place_ref[h] = place
+        hot = pick(place >> 1 == lane)
+        terms = [
+            jnp.where((place & 1) == half, jnp.where(half == h, p, r), 0.0).astype(BF16)
+            for p, r in zip(pieces, rolled)
+        ]
+        total = total + lax.dot_general(
+            hot, jnp.concatenate(terms, axis=1), TN, preferred_element_type=F32
+        )
+    predicted = total[:rows, :LANES] + total[:rows, LANES:]
     misfit = observed_ref[...] - predicted
     misfit_ref[...] = misfit
     weight = weight_ref[...]
@@ -146,7 +185,7 @@
         out_ref[s] = total
 
 
-def weighted_kernel(terms_ref, misfit_ref, weight_ref, station_ref, corr_ref, weighted_ref, out_ref):
+def weighted_kernel(terms_ref, misfit_ref, weight_ref, station_ref, place_ref, corr_ref, weighted_ref, out_ref):
     total = terms_ref[0]
     for s in range(1, terms_ref.shape[0]):
         total = total + terms_ref[s]
@@ -165,25 +204,34 @@
         found.append(jnp.sum(jnp.where(own, wide, 0.0), axis=0, keepdims=True))
     weighted = weight_ref[...] * (misfit_ref[...] - jnp.concatenate(found, axis=0))
     weighted_ref[...] = weighted
-    half = weighted.astype(BF16)
-    for s in range(out_ref.shape[0]):
-        out_ref[s] = half
-
-
-def backward_kernel(pick_ref, cell_ref, resid_ref, blocks_ref, out_ref, terms_ref):
+    halves = jnp.concatenate(
+        [weighted.astype(BF16), jnp.zeros((LANES - weighted.shape[0], LANES), BF16)], axis=0
+    )
+    lane = iota(place_ref.shape[1:], 1)
+    half = (lane >= PICK_BLK).astype(jnp.int32)
+    sent = None
+    for h in (0, 1):
+        place = place_ref[h]
+        found = jnp.dot(pick(place >> 1 == lane), halves, preferred_element_type=F32)
+        found = jnp.where((place & 1) == h, found, pltpu.roll(found, PICK_BLK, 1))
+        sent = found if h == 0 else jnp.where(half == 0, sent, found)
+    out_ref[...] = sent.astype(BF16).reshape(out_ref.shape)
+
+
+def backward_kernel(code_ref, cell_ref, resid_ref, blocks_ref, out_ref, terms_ref):
     slots = blocks_ref.shape[0]
     lane, sub = iota((CHUNK, LANES), 1), iota((CHUNK, LANES), 0)
     sub_g = iota((GROUP, LANES), 0)
     parity = sub & 1
     half = (lane >= PICK_BLK).astype(jnp.int32)
     for n in range(slots // CHUNK):
-        pick_down = down(pick_ref[n : n + 1, :])
-        row_of = pick_down >> 1
+        code_down = down(code_ref[n : n + 1, :])
+        row_of = code_down >> 1
         chosen = jnp.concatenate(
             [pick(row_of == lane + t) for t in range(0, resid_ref.shape[0], LANES)], axis=1
         )
         resid = jnp.dot(chosen, resid_ref[...], preferred_element_type=F32)
-        resid = jnp.where((pick_down & 1) == parity, resid, pltpu.roll(resid, PICK_BLK, 1))
+        resid = jnp.where((code_down & 1) == parity, resid, pltpu.roll(resid, PICK_BLK, 1))
         resid = jnp.where(half == parity, resid, 0.0)
         parts = []
         for j in range(0, CHUNK, GROUP):
@@ -248,7 +296,6 @@
     observed, weight = observed.reshape(-1, LANES), pick_weight.reshape(-1, LANES)
     station = station.reshape(-1, LANES)
     own_rows = observed.shape[0]
-    group_rows = own_rows * shells
     stat_rows = 2 * STATIONS // LANES
     shape = jax.ShapeDtypeStruct
 
@@ -256,12 +303,14 @@
     lines, planes = torus_groups()
     devices = ("events", "shells")
 
-    partials, blocks, used_picks = pl.pallas_call(
+    slots = sensitivity.shape[0]
+    q = SLOT_CAP // 2
+    partials, blocks, codes = pl.pallas_call(
         forward_kernel,
         in_specs=[outside] * 5,
         out_specs=(pl.BlockSpec(memory_space=pltpu.VMEM),) * 3,
         out_shape=(
-            shape((group_rows, LANES), F32),
+            shape((shells, SLOT_CAP + 8, LANES), BF16),
             shape(sensitivity.shape, BF16),
             shape(picks_of.shape, jnp.int32),
         ),
@@ -270,17 +319,22 @@
             pltpu.VMEM(picks_of.shape, jnp.int32),
             pltpu.VMEM(cells_of.shape, jnp.int32),
             pltpu.VMEM(model_rows.shape, BF16),
-            pltpu.VMEM((sensitivity.shape[0], 2 * LANES), BF16),
+            pltpu.VMEM((slots, 2 * LANES), BF16),
+            pltpu.VMEM((shells * q, slots), BF16),
             pltpu.SemaphoreType.DMA((4,)),
-            pltpu.SemaphoreType.DMA((sensitivity.shape[0] // CHUNK,)),
+            pltpu.SemaphoreType.DMA((8,)),
         ],
         compiler_params=pltpu.CompilerParams(vmem_limit_bytes=VMEM_BYTES),
         name="forward",
     )(blk_count, picks_of, cells_of, model_rows, sensitivity)
-    partials = swap(partials.reshape(shells, own_rows, LANES), "shells")
-    misfit, stats = simple(
+    partials = swap(partials, "shells")
+    misfit, places, stats = simple(
         stations_kernel,
-        (shape((own_rows, LANES), F32), shape((len(lines[0]), stat_rows, LANES), F32)),
+        (
+            shape((own_rows, LANES), F32),
+            shape((2, shells * q, LANES), jnp.int32),
+            shape((len(lines[0]), stat_rows, LANES), F32),
+        ),
         "stations",
     )(partials, observed, weight, station)
     stats = swap(stats, devices, lines)
@@ -291,17 +345,17 @@
         (
             shape((STATIONS // LANES, LANES), F32),
             shape((own_rows, LANES), F32),
-            shape((shells, own_rows, LANES), BF16),
+            shape((shells, q, LANES), BF16),
         ),
         "weighted",
-    )(stats, misfit, weight, station)
-    halves = swap(halves, "shells").reshape(group_rows, LANES)
+    )(stats, misfit, weight, station, places)
+    halves = swap(halves, "shells").reshape(shells * q, LANES)
     grads = simple(
         backward_kernel,
         shape((events,) + model_rows.shape, BF16),
         "backward",
         scratch_shapes=[pltpu.VMEM((sensitivity.shape[0], 2 * LANES), BF16)],
-    )(used_picks, cells_of, halves, blocks)
+    )(codes, cells_of, halves, blocks)
     grads = swap(grads, "events")
     gradient = simple(gradient_kernel, shape(model_rows.shape, F32), "gradient")(grads)
     return (gradient.reshape(-1), correction.reshape(-1), weighted.reshape(-1))

time: 109 us -> 103 us (0.945)
  blocking collectives: 95 us -> 88.3 us
    all_to_all x5, blocking collectives: 95 us -> 88.3 us  [swap(): return lax.all_to_all(x, axis, 0, 0, tiled=True, axis_index_groups=groups)]
where the time goes in v3:
time: 103 us; the launch traced here: 102 us
  blocking collectives  88.3 us (86%)
  Pallas kernels  10.5 us (10%)
  local copies, waits for them, and re-layouts  2.27 us (2%)
  between operations  1.35 us (1%)
    all_to_all x5, blocking collectives, swap(): return lax.all_to_all(x, axis, 0, 0, tiled=True, axis_index_groups=groups)  88.3 us
    pallas_call x1, Pallas kernels, local(): pl.pallas_call(forward_kernel, in_specs=[outside] * 5, out_specs=(pl.Bloc...  5.16 us
    unnamed x14, local copies, waits for them, and re-layouts  2.27 us
    pallas_call x1, Pallas kernels, local(): simple(backward_kernel, shape((events,) + model_rows.shape, BF16), 'backw...  2.24 us

profile of v3, /device:TPU:1, one launch (start us, length us, event | category | flops | bytes accessed | tf_op | source)
XLA Modules:
  0.0 102.4 jit_solution(6404454434036394523)
XLA Ops:
  0.6 0.0 copy-start.5
  1.3 0.0 copy-start
  1.3 0.9 copy-done
  2.2 0.0 copy-start.4
  2.2 0.7 copy-done.4
  2.9 0.0 copy-start.6
  2.9 0.7 copy-done.6
  3.6 0.0 copy-start.1
  3.6 0.0 copy-start.2
  3.6 0.0 copy-start.3
  3.6 5.2 %forward.1 = (bf16[32,40,128]{2,1,0:T(8,128)(2,1)S(1)}, bf16[512,64,128]{2,1,0:T(8,128)(2,1)S(1)}, s32[4,128]{1,0:T(4,128)S(1)}) custom-call(s32[1]{0:T(128)S(6)} %copy.11.count_hbm, s32[4,128]{1,0:T(4,128)S(1)} %bitcast.19, s32[4,128]{1,0:T(4,128)S(1)} %bitcast.17, bf16[512,128]{1,0:T(8,128)(2,1)S(1)} %bitcast.11, bf16[512,64,128]{2,1,0:T(8,128)(2,1)} %blocks_hbm.1), custom_call_target="tpu_custom_call" | custom-call | tf_op jit(solution)/shard_map/forward/pallas_call | solution.py:308
  8.7 27.2 %all_to_all.25.terms_ref = bf16[32,40,128]{2,1,0:T(8,128)(2,1)S(1)} all-to-all(bf16[32,40,128]{2,1,0:T(8,128)(2,1)S(1)} %get-tuple-element.13), channel_id=1, replica_groups=mesh['events'=8,'shells'=32] {'shells'}, dimensions={0} | all-to-all | bytes 655360 | tf_op jit(solution)/shard_map/all_to_all | solution.py:279
  36.0 0.0 copy-done.1
  36.0 0.0 copy-done.2
  36.0 0.0 copy-done.3
  36.0 1.1 %stations.1 = (f32[32,128]{1,0:T(8,128)S(1)}, s32[2,512,128]{2,1,0:T(8,128)S(1)}, f32[16,32,128]{2,1,0:T(8,128)S(1)}) custom-call(bf16[32,40,128]{2,1,0:T(8,128)(2,1)S(1)} %all_to_all.25.terms_ref, f32[32,128]{1,0:T(8,128)S(1)} %bitcast.16, f32[32,128]{1,0:T(8,128)S(1)} %bitcast.12, s32[32,128]{1,0:T(8,128)S(1)} %bitcast.14), custom_call_target="tpu_custom_call" | custom-call | tf_op jit(solution)/shard_map/stations/pallas_call | solution.py:331
  37.1 14.8 %all_to_all.26.terms_ref = f32[16,32,128]{2,1,0:T(8,128)S(1)} all-to-all(f32[16,32,128]{2,1,0:T(8,128)S(1)} %get-tuple-element.14), channel_id=1, replica_groups={{0,1,2,3,4,5,6,7,32,33,34,35,36,37,38,39},{8,9,10,11,12,13,14,15,40,41,..., dimensions={0} | all-to-all | bytes 524288 | tf_op jit(solution)/shard_map/all_to_all | solution.py:279
  52.0 13.1 %all_to_all.27.terms_ref = f32[16,32,128]{2,1,0:T(8,128)S(1)} all-to-all(f32[16,32,128]{2,1,0:T(8,128)S(1)} %spread.1), channel_id=1, replica_groups={{0,8,16,24,64,72,80,88,128,136,144,152,192,200,208,216},{1,9,17,25,65,7..., dimensions={0} | all-to-all | bytes 524288 | tf_op jit(solution)/shard_map/all_to_all | solution.py:279
  65.0 1.1 %weighted.1 = (f32[16,128]{1,0:T(8,128)}, f32[32,128]{1,0:T(8,128)}, bf16[32,16,128]{2,1,0:T(8,128)(2,1)S(1)}) custom-call(f32[16,32,128]{2,1,0:T(8,128)S(1)} %all_to_all.27.terms_ref, f32[32,128]{1,0:T(8,128)S(1)} %get-tuple-element.15.misfit_ref, f32[32,128]{1,0:T(8,128)S(1)} %bitcast.13, s32[32,128]{1,0:T(8,128)S(1)} %bitcast.15, ...), custom_call_target="tpu_custom_call" | custom-call | tf_op jit(solution)/shard_map/weighted/pallas_call | solution.py:343
  66.1 14.9 %all_to_all.28 = bf16[32,16,128]{2,1,0:T(8,128)(2,1)S(1)} all-to-all(bf16[32,16,128]{2,1,0:T(8,128)(2,1)S(1)} %get-tuple-element.17), channel_id=1, replica_groups=mesh['events'=8,'shells'=32] {'shells'}, dimensions={0} | all-to-all | bytes 262144 | tf_op jit(solution)/shard_map/all_to_all | solution.py:279
  81.0 0.0 copy-done.5
  81.0 2.2 %backward.1 = bf16[8,512,128]{2,1,0:T(8,128)(2,1)S(1)} custom-call(s32[4,128]{1,0:T(4,128)S(1)} %get-tuple-element.12.code_ref, s32[4,128]{1,0:T(4,128)S(1)} %bitcast.18, bf16[512,128]{1,0:T(8,128)(2,1)S(1)} %bitcast.10, bf16[512,64,128]{2,1,0:T(8,128)(2,1)S(1)} %get-tuple-element.18.blocks_ref), custom_call_target="tpu_custom_call" | custom-call | tf_op jit(solution)/shard_map/backward/pallas_call | solution.py:353
  83.3 18.3 %all_to_all.29.terms_ref = bf16[8,512,128]{2,1,0:T(8,128)(2,1)S(1)} all-to-all(bf16[8,512,128]{2,1,0:T(8,128)(2,1)S(1)} %backward.1), channel_id=1, replica_groups=mesh['events'=8,'shells'=32] {'events'}, dimensions={0} | all-to-all | bytes 2097152 | tf_op jit(solution)/shard_map/all_to_all | solution.py:279
  101.6 0.8 gradient.1
  (1 shorter events, 0.0 us)
Async XLA Ops:
  0.6 80.4 %copy-start.5 = (s32[512]{0:T(512)S(1)}, s32[512]{0:T(512)}, u32[]{:S(2)}) copy-start(s32[512]{0:T(512)} %param.11) | copy-start | bytes 6148
  1.3 0.9 copy-start
  2.2 0.7 copy-start.4
  2.9 0.7 copy-start.6
  3.6 32.4 %copy-start.1 = (f32[4096]{0:T(1024)S(1)}, f32[4096]{0:T(1024)}, u32[]{:S(2)}) copy-start(f32[4096]{0:T(1024)} %param.14) | copy-start | bytes 49156
  3.6 32.4 %copy-start.2 = (s32[4096]{0:T(1024)S(1)}, s32[4096]{0:T(1024)}, u32[]{:S(2)}) copy-start(s32[4096]{0:T(1024)} %param.15) | copy-start | bytes 49156
  3.6 32.4 %copy-start.3 = (f32[4096]{0:T(1024)S(1)}, f32[4096]{0:T(1024)}, u32[]{:S(2)}) copy-start(f32[4096]{0:T(1024)} %param.13) | copy-start | bytes 49156

commit v4 on v3

--- a/solution.py
+++ b/solution.py
@@ -90,10 +90,12 @@
         cell_down = down(cell_ref[n : n + 1, :])
         chosen = jnp.concatenate([pick(cell_down == lane + t) for t in range(0, cells, LANES)], axis=1)
         rows.append(jnp.dot(chosen, model_ref[...], preferred_element_type=F32))
-        tagged = jnp.logical_and(iota((owners * 8, LANES), 0) >> 3 == owner, used)
-        tagged = jnp.where(tagged, (inside + 1).astype(F32), 0.0).astype(BF16)
-        ranked = pick((code_down[n] & (SLOT_CAP - 1)) == lane)
-        index = index + jnp.dot(tagged, ranked, preferred_element_type=F32)
+        tile_row = jnp.where(used, owner * 8 + ((code >> 1) & 7), -1)
+        block = (inside & 1) * 32 + (inside >> 1) + 1
+        tagged = iota((owners * 8, LANES), 0) == tile_row
+        tagged = jnp.where(tagged, block.astype(F32), 0.0).astype(BF16)
+        quarter = (code_down[n] & 1) * 2 + ((code_down[n] >> 4) & 1)
+        index = index + jnp.dot(tagged, pick(lane >> 5 == quarter), preferred_element_type=F32)
         hot_ref[:, n * CHUNK : (n + 1) * CHUNK] = pick(iota((hot_ref.shape[0], LANES), 0) == code >> 1)
     out_ref[:, SLOT_CAP:, :] = index.astype(BF16).reshape(owners, 8, LANES)
 
@@ -125,31 +127,33 @@
     out_ref[:, q : 2 * q, :] = placed[:, LANES:].reshape(owners, q, LANES)
 
 
-def stations_kernel(terms_ref, observed_ref, weight_ref, station_ref, misfit_ref, place_ref, out_ref):
-    senders, rows = terms_ref.shape[0], observed_ref.shape[0]
+def row_matches(terms_ref):
+    tile = terms_ref[:, SLOT_CAP:, :].astype(F32).reshape(-1, LANES)
+    lane = (iota(tile.shape, 1) & 31).astype(F32)
+    return pick(tile == lane + 1.0), pick(tile == lane + 33.0)
+
+
+def stations_kernel(terms_ref, observed_ref, weight_ref, station_ref, misfit_ref, out_ref):
+    rows = observed_ref.shape[0]
     q = SLOT_CAP // 2
-    flat = senders * q
-    lane, sub = iota((flat, LANES), 1), iota((flat, LANES), 0)
-    half = (lane >= PICK_BLK).astype(jnp.int32)
-    index = terms_ref[:, SLOT_CAP:, :].astype(F32)
-    index = jnp.concatenate([index] * (q // 8), axis=1).reshape(flat, LANES)
-    every = jnp.ones((LANES, LANES), BF16)
-    total = jnp.zeros((LANES, 2 * LANES), F32)
-    pieces = [terms_ref[:, n * q : (n + 1) * q, :].astype(F32).reshape(flat, LANES) for n in (0, 1)]
-    rolled = [pltpu.roll(p, PICK_BLK, 1) for p in pieces]
-    for h in (0, 1):
-        own = jnp.where(lane == 2 * (sub & (q - 1)) + h, index, 0.0).astype(BF16)
-        place = jnp.dot(own, every, preferred_element_type=F32).astype(jnp.int32) - 1
-        place_ref[h] = place
-        hot = pick(place >> 1 == lane)
-        terms = [
-            jnp.where((place & 1) == half, jnp.where(half == h, p, r), 0.0).astype(BF16)
-            for p, r in zip(pieces, rolled)
-        ]
-        total = total + lax.dot_general(
-            hot, jnp.concatenate(terms, axis=1), TN, preferred_element_type=F32
-        )
-    predicted = total[:rows, :LANES] + total[:rows, LANES:]
+
+    def part(first):
+        return terms_ref[:, first : first + 8, :].astype(F32).reshape(-1, LANES).astype(BF16)
+
+    lower, upper = [jnp.concatenate([part(t), part(q + t)], axis=1) for t in (0, 8)]
+    sides = []
+    for match in row_matches(terms_ref):
+        low_sum = lax.dot_general(match, lower, TN, preferred_element_type=F32)
+        top_sum = lax.dot_general(match, upper, TN, preferred_element_type=F32)
+        low_sum = low_sum[:, :LANES] + low_sum[:, LANES:]
+        top_sum = top_sum[:, :LANES] + top_sum[:, LANES:]
+        sides.append((low_sum[0:32] + top_sum[32:64], low_sum[64:96] + top_sum[96:128]))
+    (even_left, even_right), (odd_left, odd_right) = sides
+    predicted = jnp.where(
+        iota((rows, LANES), 1) < PICK_BLK,
+        even_left + pltpu.roll(even_right, PICK_BLK, 1),
+        odd_right + pltpu.roll(odd_left, PICK_BLK, 1),
+    )
     misfit = observed_ref[...] - predicted
     misfit_ref[...] = misfit
     weight = weight_ref[...]
@@ -172,9 +176,8 @@
     h = hi_count
     numer = total[0:h] + total[h : 2 * h] + total[2 * h : 3 * h]
     denom = total[3 * h : 4 * h] + total[4 * h : 5 * h] + total[5 * h : 6 * h]
-    sums = jnp.concatenate([numer, denom], axis=0)
     for s in range(out_ref.shape[0]):
-        out_ref[s] = sums
+        out_ref[s] = denom if s % 2 else numer
 
 
 def spread_kernel(terms_ref, out_ref):
@@ -185,37 +188,38 @@
         out_ref[s] = total
 
 
-def weighted_kernel(terms_ref, misfit_ref, weight_ref, station_ref, place_ref, corr_ref, weighted_ref, out_ref):
-    total = terms_ref[0]
-    for s in range(1, terms_ref.shape[0]):
-        total = total + terms_ref[s]
-    hi_count = STATIONS // LANES
-    corr = total[:hi_count] / (total[hi_count:] + 1.0)
+def weighted_kernel(terms_ref, misfit_ref, weight_ref, station_ref, partials_ref, corr_ref, weighted_ref, out_ref):
+    numer, denom = terms_ref[0], terms_ref[1]
+    for s in range(2, terms_ref.shape[0], 2):
+        numer = numer + terms_ref[s]
+        denom = denom + terms_ref[s + 1]
+    corr = numer / (denom + 1.0)
     corr_ref[...] = corr
     stations = station_ref[...]
     high, low = stations >> 7, stations & (LANES - 1)
-    table = jnp.concatenate(three_parts(corr), axis=0)
-    found = []
-    for r in range(stations.shape[0]):
-        hot = pick(iota((LANES, LANES), 0) == low[r : r + 1])
-        wide = jnp.dot(table, hot, preferred_element_type=F32)
-        wide = (wide[:hi_count] + wide[hi_count : 2 * hi_count]) + wide[2 * hi_count :]
-        own = iota((hi_count, LANES), 0) == high[r : r + 1]
-        found.append(jnp.sum(jnp.where(own, wide, 0.0), axis=0, keepdims=True))
-    weighted = weight_ref[...] * (misfit_ref[...] - jnp.concatenate(found, axis=0))
+    found = jnp.zeros(stations.shape, F32)
+    for h in range(corr.shape[0]):
+        line = jnp.broadcast_to(corr[h : h + 1], stations.shape)
+        found = jnp.where(high == h, jnp.take_along_axis(line, low, axis=1), found)
+    weighted = weight_ref[...] * (misfit_ref[...] - found)
     weighted_ref[...] = weighted
-    halves = jnp.concatenate(
-        [weighted.astype(BF16), jnp.zeros((LANES - weighted.shape[0], LANES), BF16)], axis=0
-    )
-    lane = iota(place_ref.shape[1:], 1)
-    half = (lane >= PICK_BLK).astype(jnp.int32)
-    sent = None
-    for h in (0, 1):
-        place = place_ref[h]
-        found = jnp.dot(pick(place >> 1 == lane), halves, preferred_element_type=F32)
-        found = jnp.where((place & 1) == h, found, pltpu.roll(found, PICK_BLK, 1))
-        sent = found if h == 0 else jnp.where(half == 0, sent, found)
-    out_ref[...] = sent.astype(BF16).reshape(out_ref.shape)
+    halves = weighted.astype(BF16).astype(F32)
+    lane = iota(halves.shape, 1)
+    left = lane < PICK_BLK
+    turned = pltpu.roll(halves, PICK_BLK, 1)
+    none = jnp.zeros_like(halves)
+    tables = []
+    for both in (jnp.where(left, halves, turned), jnp.where(left, turned, halves)):
+        first, second = jnp.where(left, both, 0.0), jnp.where(left, 0.0, both)
+        lower = jnp.concatenate([first, none, second, none], axis=0)
+        upper = jnp.concatenate([none, first, none, second], axis=0)
+        tables.append(jnp.concatenate([lower, upper], axis=1))
+    table = jnp.concatenate(tables, axis=0).astype(BF16)
+    matches = jnp.concatenate(row_matches(partials_ref), axis=1)
+    sent = jnp.dot(matches, table, preferred_element_type=F32)
+    peers = out_ref.shape[0]
+    sent = [sent[:, t : t + LANES].reshape(peers, 8, LANES) for t in (0, LANES)]
+    out_ref[...] = jnp.concatenate(sent, axis=1).astype(BF16)
 
 
 def backward_kernel(code_ref, cell_ref, resid_ref, blocks_ref, out_ref, terms_ref):
@@ -258,11 +262,20 @@
             out_ref[s, t : t + tile, :] = sums
 
 
-def gradient_kernel(terms_ref, out_ref):
-    total = terms_ref[0].astype(F32)
-    for s in range(1, terms_ref.shape[0]):
-        total = total + terms_ref[s].astype(F32)
-    out_ref[...] = total
+def gradient_kernel(terms_ref, out_hbm, total_ref, sems):
+    pieces = sems.shape[0]
+    rows = total_ref.shape[0] // pieces
+    copies = []
+    for n in range(pieces):
+        at = pl.ds(n * rows, rows)
+        total = terms_ref[0, at, :].astype(F32)
+        for s in range(1, terms_ref.shape[0]):
+            total = total + terms_ref[s, at, :].astype(F32)
+        total_ref[at, :] = total
+        copies.append(pltpu.make_async_copy(total_ref.at[at], out_hbm.at[at], sems.at[n]))
+        copies[-1].start()
+    for copy in copies:
+        copy.wait()
 
 
 def simple(kernel, out_shape, name, **more):
@@ -284,7 +297,7 @@
     for x, zl, y, zh, c in itertools.product(range(4), range(2), range(4), range(4), range(2)):
         flat = (x * 2 + zl) * 32 + y * 8 + zh * 2 + c
         lines.setdefault((x, y), []).append(flat)
-        planes.setdefault((zl, zh, c), []).append(flat)
+        planes.setdefault((zl, zh), []).append(flat)
     return list(lines.values()), list(planes.values())
 
 
@@ -296,7 +309,7 @@
     observed, weight = observed.reshape(-1, LANES), pick_weight.reshape(-1, LANES)
     station = station.reshape(-1, LANES)
     own_rows = observed.shape[0]
-    stat_rows = 2 * STATIONS // LANES
+    stat_rows = STATIONS // LANES
     shape = jax.ShapeDtypeStruct
 
     outside = pl.BlockSpec(memory_space=pltpu.HBM)
@@ -326,13 +339,18 @@
         ],
         compiler_params=pltpu.CompilerParams(vmem_limit_bytes=VMEM_BYTES),
         name="forward",
-    )(blk_count, picks_of, cells_of, model_rows, sensitivity)
+    )(
+        blk_count,
+        *[
+            pltpu.with_memory_space_constraint(v, pltpu.HBM)
+            for v in (picks_of, cells_of, model_rows, sensitivity)
+        ],
+    )
     partials = swap(partials, "shells")
-    misfit, places, stats = simple(
+    misfit, stats = simple(
         stations_kernel,
         (
             shape((own_rows, LANES), F32),
-            shape((2, shells * q, LANES), jnp.int32),
             shape((len(lines[0]), stat_rows, LANES), F32),
         ),
         "stations",
@@ -348,7 +366,7 @@
             shape((shells, q, LANES), BF16),
         ),
         "weighted",
-    )(stats, misfit, weight, station, places)
+    )(stats, misfit, weight, station, partials)
     halves = swap(halves, "shells").reshape(shells * q, LANES)
     grads = simple(
         backward_kernel,
@@ -357,7 +375,13 @@
         scratch_shapes=[pltpu.VMEM((sensitivity.shape[0], 2 * LANES), BF16)],
     )(codes, cells_of, halves, blocks)
     grads = swap(grads, "events")
-    gradient = simple(gradient_kernel, shape(model_rows.shape, F32), "gradient")(grads)
+    gradient = simple(
+        gradient_kernel,
+        shape(model_rows.shape, F32),
+        "gradient",
+        out_specs=outside,
+        scratch_shapes=[pltpu.VMEM(model_rows.shape, F32), pltpu.SemaphoreType.DMA((4,))],
+    )(grads)
     return (gradient.reshape(-1), correction.reshape(-1), weighted.reshape(-1))
 
 

time: 103 us -> 100 us (0.971)
  blocking collectives: 88.3 us -> 85.8 us
  local copies, waits for them, and re-layouts: 2.27 us -> 0.02 us
  Pallas kernels: 10.5 us -> 12.5 us
    all_to_all x5, blocking collectives: 88.3 us -> 85.8 us  [swap(): return lax.all_to_all(x, axis, 0, 0, tiled=True, axis_index_groups=groups)]
    pallas_call x1, Pallas kernels: 5.16 us -> 7.68 us  [local(): pl.pallas_call(forward_kernel, in_specs=[outside] * 5, out_specs=(pl.Bloc...]
    unnamed x14 -> x8, local copies, waits for them, and re-layouts: 2.27 us -> 0.02 us
where the time goes in v4:
time: 100 us; the launch traced here: 99.7 us
  blocking collectives  85.8 us (86%)
  Pallas kernels  12.5 us (12%)
  between operations  1.37 us (1%)
    all_to_all x5, blocking collectives, swap(): return lax.all_to_all(x, axis, 0, 0, tiled=True, axis_index_groups=groups)  85.8 us
    pallas_call x1, Pallas kernels, local(): pl.pallas_call(forward_kernel, in_specs=[outside] * 5, out_specs=(pl.Bloc...  7.68 us
    pallas_call x1, Pallas kernels, local(): simple(backward_kernel, shape((events,) + model_rows.shape, BF16), 'backw...  2.24 us

profile of v4, /device:TPU:1, one launch (start us, length us, event | category | flops | bytes accessed | tf_op | source)
XLA Modules:
  0.0 99.7 jit_solution(13385519780448366173)
XLA Ops:
  0.6 0.0 copy-start.3
  0.6 0.0 copy-start.1
  0.7 0.0 copy-start
  0.7 0.0 copy-start.2
  1.3 7.7 %forward.1 = (bf16[32,40,128]{2,1,0:T(8,128)(2,1)S(1)}, bf16[512,64,128]{2,1,0:T(8,128)(2,1)S(1)}, s32[4,128]{1,0:T(4,128)S(1)}) custom-call(s32[1]{0:T(128)S(6)} %copy.11.count_hbm, s32[4,128]{1,0:T(4,128)} %bitcast.20, s32[4,128]{1,0:T(4,128)} %bitcast.16, bf16[512,128]{1,0:T(8,128)(2,1)} %bitcast.19, bf16[512,64,128]{2,1,0:T(8,128)(2,1)} %blocks_hbm.1), custom_call_target="tpu_custom_call" | custom-call | tf_op jit(solution)/shard_map/forward/pallas_call | solution.py:321
  9.0 27.3 %all_to_all.25.terms_ref.partials_ref = bf16[32,40,128]{2,1,0:T(8,128)(2,1)S(1)} all-to-all(bf16[32,40,128]{2,1,0:T(8,128)(2,1)S(1)} %get-tuple-element.12), channel_id=1, replica_groups=mesh['events'=8,'shells'=32] {'shells'}, dimensions={0} | all-to-all | bytes 655360 | tf_op jit(solution)/shard_map/all_to_all | solution.py:292
  36.3 0.0 copy-done.1
  36.3 0.0 copy-done
  36.3 0.0 copy-done.2
  36.3 0.8 stations.1
  37.1 12.0 %all_to_all.26.terms_ref = f32[16,16,128]{2,1,0:T(8,128)S(1)} all-to-all(f32[16,16,128]{2,1,0:T(8,128)S(1)} %get-tuple-element.13), channel_id=1, replica_groups={{0,1,2,3,4,5,6,7,32,33,34,35,36,37,38,39},{8,9,10,11,12,13,14,15,40,41,..., dimensions={0} | all-to-all | bytes 262144 | tf_op jit(solution)/shard_map/all_to_all | solution.py:292
  49.2 14.0 %all_to_all.27.terms_ref = f32[32,16,128]{2,1,0:T(8,128)S(1)} all-to-all(f32[32,16,128]{2,1,0:T(8,128)S(1)} %spread.1), channel_id=1, replica_groups={{0,1,8,9,16,17,24,25,64,65,72,73,80,81,88,89,128,129,136,137,144,145,15..., dimensions={0} | all-to-all | bytes 524288 | tf_op jit(solution)/shard_map/all_to_all | solution.py:292
  63.2 1.0 weighted.1
  64.1 14.4 %all_to_all.28 = bf16[32,16,128]{2,1,0:T(8,128)(2,1)S(1)} all-to-all(bf16[32,16,128]{2,1,0:T(8,128)(2,1)S(1)} %get-tuple-element.15), channel_id=1, replica_groups=mesh['events'=8,'shells'=32] {'shells'}, dimensions={0} | all-to-all | bytes 262144 | tf_op jit(solution)/shard_map/all_to_all | solution.py:292
  78.5 0.0 copy-done.3
  78.5 2.2 %backward.1 = bf16[8,512,128]{2,1,0:T(8,128)(2,1)S(1)} custom-call(s32[4,128]{1,0:T(4,128)S(1)} %get-tuple-element.11.code_ref, s32[4,128]{1,0:T(4,128)S(1)} %bitcast.17, bf16[512,128]{1,0:T(8,128)(2,1)S(1)} %bitcast.10, bf16[512,64,128]{2,1,0:T(8,128)(2,1)S(1)} %get-tuple-element.16.blocks_ref), custom_call_target="tpu_custom_call" | custom-call | tf_op jit(solution)/shard_map/backward/pallas_call | solution.py:371
  80.7 18.2 %all_to_all.29.terms_ref = bf16[8,512,128]{2,1,0:T(8,128)(2,1)S(1)} all-to-all(bf16[8,512,128]{2,1,0:T(8,128)(2,1)S(1)} %backward.1), channel_id=1, replica_groups=mesh['events'=8,'shells'=32] {'events'}, dimensions={0} | all-to-all | bytes 2097152 | tf_op jit(solution)/shard_map/all_to_all | solution.py:292
  98.9 0.8 gradient.1
  (1 shorter events, 0.0 us)
Async XLA Ops:
  0.6 77.9 %copy-start.3 = (s32[512]{0:T(512)S(1)}, s32[512]{0:T(512)}, u32[]{:S(2)}) copy-start(s32[512]{0:T(512)} %param.11) | copy-start | bytes 6148
  0.6 35.6 %copy-start.1 = (s32[4096]{0:T(1024)S(1)}, s32[4096]{0:T(1024)}, u32[]{:S(2)}) copy-start(s32[4096]{0:T(1024)} %param.15) | copy-start | bytes 49156
  0.7 35.6 %copy-start = (f32[4096]{0:T(1024)S(1)}, f32[4096]{0:T(1024)}, u32[]{:S(2)}) copy-start(f32[4096]{0:T(1024)} %param.14) | copy-start | bytes 49156
  0.7 35.6 %copy-start.2 = (f32[4096]{0:T(1024)S(1)}, f32[4096]{0:T(1024)}, u32[]{:S(2)}) copy-start(f32[4096]{0:T(1024)} %param.13) | copy-start | bytes 49156

commit v5 on v4

--- a/solution.py
+++ b/solution.py
@@ -59,12 +59,17 @@
     ]
     for copy in tables:
         copy.start()
-    copies = []
     piece = slots // block_sems.shape[0]
-    for n in range(slots // piece):
+
+    def block_copy(n):
         at = pl.ds(n * piece, piece)
-        copies.append(pltpu.make_async_copy(blocks_hbm.at[at], blocks_ref.at[at], block_sems.at[n]))
-        copies[-1].start()
+        return pltpu.make_async_copy(blocks_hbm.at[at], blocks_ref.at[at], block_sems.at[n])
+
+    def start_copy(n, carry):
+        block_copy(n).start()
+        return carry
+
+    lax.fori_loop(0, slots // piece, start_copy, 0)
     for copy in tables:
         copy.wait()
     lane, sub = iota((CHUNK, LANES), 1), iota((CHUNK, LANES), 0)
@@ -105,7 +110,7 @@
         for j in range(0, CHUNK, GROUP):
             first = n * CHUNK + j
             if first % piece == 0:
-                copies[first // piece].wait()
+                block_copy(first // piece).wait()
             block = blocks_ref[first : first + GROUP].reshape(GROUP * PICK_BLK, CELL_BLK)
             wide = lax.dot_general(
                 rows[n][j : j + GROUP].astype(BF16), block, NT, preferred_element_type=F32
@@ -222,7 +227,14 @@
     out_ref[...] = jnp.concatenate(sent, axis=1).astype(BF16)
 
 
-def backward_kernel(code_ref, cell_ref, resid_ref, blocks_ref, out_ref, terms_ref):
+def backward_kernel(code_ref, cell_ref, resid_ref, blocks_ref, corr_ref, weighted_ref,
+                    out_ref, corr_hbm, weighted_hbm, terms_ref, sems):
+    copies = [
+        pltpu.make_async_copy(corr_ref, corr_hbm, sems.at[0]),
+        pltpu.make_async_copy(weighted_ref, weighted_hbm, sems.at[1]),
+    ]
+    for copy in copies:
+        copy.start()
     slots = blocks_ref.shape[0]
     lane, sub = iota((CHUNK, LANES), 1), iota((CHUNK, LANES), 0)
     sub_g = iota((GROUP, LANES), 0)
@@ -260,6 +272,8 @@
         sums = (sums[:, :LANES] + sums[:, LANES:]).astype(BF16)
         for s in range(out_ref.shape[0]):
             out_ref[s, t : t + tile, :] = sums
+    for copy in copies:
+        copy.wait()
 
 
 def gradient_kernel(terms_ref, out_hbm, total_ref, sems):
@@ -335,7 +349,7 @@
             pltpu.VMEM((slots, 2 * LANES), BF16),
             pltpu.VMEM((shells * q, slots), BF16),
             pltpu.SemaphoreType.DMA((4,)),
-            pltpu.SemaphoreType.DMA((8,)),
+            pltpu.SemaphoreType.DMA((16,)),
         ],
         compiler_params=pltpu.CompilerParams(vmem_limit_bytes=VMEM_BYTES),
         name="forward",
@@ -368,12 +382,18 @@
         "weighted",
     )(stats, misfit, weight, station, partials)
     halves = swap(halves, "shells").reshape(shells * q, LANES)
-    grads = simple(
+    vmem = pl.BlockSpec(memory_space=pltpu.VMEM)
+    grads, correction, weighted = simple(
         backward_kernel,
-        shape((events,) + model_rows.shape, BF16),
+        (
+            shape((events,) + model_rows.shape, BF16),
+            shape(correction.shape, F32),
+            shape(weighted.shape, F32),
+        ),
         "backward",
-        scratch_shapes=[pltpu.VMEM((sensitivity.shape[0], 2 * LANES), BF16)],
-    )(codes, cells_of, halves, blocks)
+        out_specs=(vmem, outside, outside),
+        scratch_shapes=[pltpu.VMEM((slots, 2 * LANES), BF16), pltpu.SemaphoreType.DMA((2,))],
+    )(codes, cells_of, halves, blocks, correction, weighted)
     grads = swap(grads, "events")
     gradient = simple(
         gradient_kernel,

time: 100 us -> 98.4 us (0.984)
  Pallas kernels: 12.5 us -> 11 us
    pallas_call x1, Pallas kernels: 7.68 us -> 6.51 us  [local(): pl.pallas_call(forward_kernel, in_specs=[outside] * 5, out_specs=(pl.Bloc...]
where the time goes in v5:
time: 98.4 us; the launch traced here: 98.1 us
  blocking collectives  85.7 us (87%)
  Pallas kernels  11 us (11%)
  between operations  1.38 us (1%)
    all_to_all x5, blocking collectives, swap(): return lax.all_to_all(x, axis, 0, 0, tiled=True, axis_index_groups=groups)  85.7 us
    pallas_call x1, Pallas kernels, local(): pl.pallas_call(forward_kernel, in_specs=[outside] * 5, out_specs=(pl.Bloc...  6.51 us
    pallas_call x1, Pallas kernels, local(): simple(backward_kernel, (shape((events,) + model_rows.shape, BF16), shape...  2.27 us

profile of v5, /device:TPU:1, one launch (start us, length us, event | category | flops | bytes accessed | tf_op | source)
XLA Modules:
  0.0 98.1 jit_solution(2940324922162744006)
XLA Ops:
  0.6 0.0 copy-start.3
  0.6 0.0 copy-start.1
  0.7 0.0 copy-start
  0.7 0.0 copy-start.2
  1.3 6.5 %forward.1 = (bf16[32,40,128]{2,1,0:T(8,128)(2,1)S(1)}, bf16[512,64,128]{2,1,0:T(8,128)(2,1)S(1)}, s32[4,128]{1,0:T(4,128)S(1)}) custom-call(s32[1]{0:T(128)S(6)} %copy.11.count_hbm, s32[4,128]{1,0:T(4,128)} %bitcast.20, s32[4,128]{1,0:T(4,128)} %bitcast.16, bf16[512,128]{1,0:T(8,128)(2,1)} %bitcast.19, bf16[512,64,128]{2,1,0:T(8,128)(2,1)} %blocks_hbm.1), custom_call_target="tpu_custom_call" | custom-call | tf_op jit(solution)/shard_map/forward/pallas_call | solution.py:335
  7.9 27.3 %all_to_all.25.terms_ref.partials_ref = bf16[32,40,128]{2,1,0:T(8,128)(2,1)S(1)} all-to-all(bf16[32,40,128]{2,1,0:T(8,128)(2,1)S(1)} %get-tuple-element.15), channel_id=1, replica_groups=mesh['events'=8,'shells'=32] {'shells'}, dimensions={0} | all-to-all | bytes 655360 | tf_op jit(solution)/shard_map/all_to_all | solution.py:306
  35.1 0.0 copy-done.1
  35.1 0.0 copy-done
  35.1 0.0 copy-done.2
  35.1 0.8 stations.1
  36.0 12.0 %all_to_all.26.terms_ref = f32[16,16,128]{2,1,0:T(8,128)S(1)} all-to-all(f32[16,16,128]{2,1,0:T(8,128)S(1)} %get-tuple-element.16), channel_id=1, replica_groups={{0,1,2,3,4,5,6,7,32,33,34,35,36,37,38,39},{8,9,10,11,12,13,14,15,40,41,..., dimensions={0} | all-to-all | bytes 262144 | tf_op jit(solution)/shard_map/all_to_all | solution.py:306
  48.0 14.0 %all_to_all.27.terms_ref = f32[32,16,128]{2,1,0:T(8,128)S(1)} all-to-all(f32[32,16,128]{2,1,0:T(8,128)S(1)} %spread.1), channel_id=1, replica_groups={{0,1,8,9,16,17,24,25,64,65,72,73,80,81,88,89,128,129,136,137,144,145,15..., dimensions={0} | all-to-all | bytes 524288 | tf_op jit(solution)/shard_map/all_to_all | solution.py:306
  62.0 0.5 weighted.1
  62.5 14.4 %all_to_all.28 = bf16[32,16,128]{2,1,0:T(8,128)(2,1)S(1)} all-to-all(bf16[32,16,128]{2,1,0:T(8,128)(2,1)S(1)} %get-tuple-element.18), channel_id=1, replica_groups=mesh['events'=8,'shells'=32] {'shells'}, dimensions={0} | all-to-all | bytes 262144 | tf_op jit(solution)/shard_map/all_to_all | solution.py:306
  76.9 0.0 copy-done.3
  76.9 2.3 %backward.1 = (bf16[8,512,128]{2,1,0:T(8,128)(2,1)S(1)}, f32[16,128]{1,0:T(8,128)}, f32[32,128]{1,0:T(8,128)}) custom-call(s32[4,128]{1,0:T(4,128)S(1)} %get-tuple-element.14.code_ref, s32[4,128]{1,0:T(4,128)S(1)} %bitcast.17, bf16[512,128]{1,0:T(8,128)(2,1)S(1)} %bitcast.10, bf16[512,64,128]{2,1,0:T(8,128)(2,1)S(1)} %get-tuple-element.19.blocks_ref, ...), custom_call_target="tpu_custom_call" | custom-call | tf_op jit(solution)/shard_map/backward/pallas_call | solution.py:386
  79.1 18.2 %all_to_all.29.terms_ref = bf16[8,512,128]{2,1,0:T(8,128)(2,1)S(1)} all-to-all(bf16[8,512,128]{2,1,0:T(8,128)(2,1)S(1)} %get-tuple-element.22), channel_id=1, replica_groups=mesh['events'=8,'shells'=32] {'events'}, dimensions={0} | all-to-all | bytes 2097152 | tf_op jit(solution)/shard_map/all_to_all | solution.py:306
  97.3 0.8 gradient.1
  (1 shorter events, 0.0 us)
Async XLA Ops:
  0.6 76.2 %copy-start.3 = (s32[512]{0:T(512)S(1)}, s32[512]{0:T(512)}, u32[]{:S(2)}) copy-start(s32[512]{0:T(512)} %param.11) | copy-start | bytes 6148
  0.6 34.5 %copy-start.1 = (s32[4096]{0:T(1024)S(1)}, s32[4096]{0:T(1024)}, u32[]{:S(2)}) copy-start(s32[4096]{0:T(1024)} %param.15) | copy-start | bytes 49156
  0.7 34.5 %copy-start = (f32[4096]{0:T(1024)S(1)}, f32[4096]{0:T(1024)}, u32[]{:S(2)}) copy-start(f32[4096]{0:T(1024)} %param.14) | copy-start | bytes 49156
  0.7 34.5 %copy-start.2 = (f32[4096]{0:T(1024)S(1)}, f32[4096]{0:T(1024)}, u32[]{:S(2)}) copy-start(f32[4096]{0:T(1024)} %param.13) | copy-start | bytes 49156

commit v6 on v5

--- a/solution.py
+++ b/solution.py
@@ -19,6 +19,8 @@
 TN = (((0,), (0,)), ((), ()))
 SLOT_CAP = 32
 VMEM_BYTES = 40 << 20
+OUTSIDE = pl.BlockSpec(memory_space=pltpu.HBM)
+INSIDE = pl.BlockSpec(memory_space=pltpu.VMEM)
 
 
 def iota(shape, axis):
@@ -47,7 +49,7 @@
 
 
 def forward_kernel(count_hbm, pick_hbm, cell_hbm, model_hbm, blocks_hbm, out_ref, blocks_ref, code_ref,
-                   count, pick_ref, cell_ref, model_ref, values_ref, hot_ref, table_sems, block_sems):
+                   count, pick_ref, cell_ref, model_ref, values_ref, hot_ref, table_sems, block_sem):
     slots, cells = blocks_ref.shape[0], model_ref.shape[0]
     owners = out_ref.shape[0]
     chunks = range(slots // CHUNK)
@@ -59,17 +61,8 @@
     ]
     for copy in tables:
         copy.start()
-    piece = slots // block_sems.shape[0]
-
-    def block_copy(n):
-        at = pl.ds(n * piece, piece)
-        return pltpu.make_async_copy(blocks_hbm.at[at], blocks_ref.at[at], block_sems.at[n])
-
-    def start_copy(n, carry):
-        block_copy(n).start()
-        return carry
-
-    lax.fori_loop(0, slots // piece, start_copy, 0)
+    block_copy = pltpu.make_async_copy(blocks_hbm, blocks_ref, block_sem)
+    block_copy.start()
     for copy in tables:
         copy.wait()
     lane, sub = iota((CHUNK, LANES), 1), iota((CHUNK, LANES), 0)
@@ -105,12 +98,11 @@
     out_ref[:, SLOT_CAP:, :] = index.astype(BF16).reshape(owners, 8, LANES)
 
     lane_g, sub_g = iota((GROUP, LANES), 1), iota((GROUP, LANES), 0)
+    block_copy.wait()
     for n in chunks:
         parts = []
         for j in range(0, CHUNK, GROUP):
             first = n * CHUNK + j
-            if first % piece == 0:
-                block_copy(first // piece).wait()
             block = blocks_ref[first : first + GROUP].reshape(GROUP * PICK_BLK, CELL_BLK)
             wide = lax.dot_general(
                 rows[n][j : j + GROUP].astype(BF16), block, NT, preferred_element_type=F32
@@ -237,7 +229,7 @@
         copy.start()
     slots = blocks_ref.shape[0]
     lane, sub = iota((CHUNK, LANES), 1), iota((CHUNK, LANES), 0)
-    sub_g = iota((GROUP, LANES), 0)
+    sub_p = iota((2 * GROUP, LANES), 0) & (GROUP - 1)
     parity = sub & 1
     half = (lane >= PICK_BLK).astype(jnp.int32)
     for n in range(slots // CHUNK):
@@ -250,13 +242,18 @@
         resid = jnp.where((code_down & 1) == parity, resid, pltpu.roll(resid, PICK_BLK, 1))
         resid = jnp.where(half == parity, resid, 0.0)
         parts = []
-        for j in range(0, CHUNK, GROUP):
-            block = blocks_ref[n * CHUNK + j : n * CHUNK + j + GROUP].reshape(GROUP * PICK_BLK, CELL_BLK)
-            mine = resid[j : j + GROUP]
+        for j in range(0, CHUNK, 2 * GROUP):
+            first = n * CHUNK + j
+            both = [
+                blocks_ref[k : k + GROUP].reshape(GROUP * PICK_BLK, CELL_BLK)
+                for k in (first, first + GROUP)
+            ]
+            mine = resid[j : j + 2 * GROUP]
             wide = jnp.concatenate(
-                [jnp.where(sub_g >> 1 == i, mine, 0.0) for i in range(GROUP // 2)], axis=1
+                [jnp.where((sub_p >> 1) == i, mine, 0.0) for i in range(GROUP // 2)], axis=1
             ).astype(BF16)
-            parts.append(jnp.dot(wide, block, preferred_element_type=F32))
+            terms = jnp.dot(wide, jnp.concatenate(both, axis=1), preferred_element_type=F32)
+            parts += [terms[:GROUP, :LANES], terms[GROUP:, LANES:]]
         high, low = two_parts(jnp.concatenate(parts, axis=0))
         terms_ref[n * CHUNK : (n + 1) * CHUNK, 0:LANES] = high
         terms_ref[n * CHUNK : (n + 1) * CHUNK, LANES : 2 * LANES] = low
@@ -315,6 +312,38 @@
     return list(lines.values()), list(planes.values())
 
 
+def forward_call(count, picks_of, cells_of, model_rows, sensitivity, shells):
+    slots = sensitivity.shape[0]
+    return pl.pallas_call(
+        forward_kernel,
+        in_specs=[OUTSIDE] * 5,
+        out_specs=(INSIDE,) * 3,
+        out_shape=(
+            jax.ShapeDtypeStruct((shells, SLOT_CAP + 8, LANES), BF16),
+            jax.ShapeDtypeStruct(sensitivity.shape, BF16),
+            jax.ShapeDtypeStruct(picks_of.shape, jnp.int32),
+        ),
+        scratch_shapes=[
+            pltpu.SMEM((1,), jnp.int32),
+            pltpu.VMEM(picks_of.shape, jnp.int32),
+            pltpu.VMEM(cells_of.shape, jnp.int32),
+            pltpu.VMEM(model_rows.shape, BF16),
+            pltpu.VMEM((slots, 2 * LANES), BF16),
+            pltpu.VMEM((shells * SLOT_CAP // 2, slots), BF16),
+            pltpu.SemaphoreType.DMA((4,)),
+            pltpu.SemaphoreType.DMA,
+        ],
+        compiler_params=pltpu.CompilerParams(vmem_limit_bytes=VMEM_BYTES),
+        name="forward",
+    )(
+        count,
+        *[
+            pltpu.with_memory_space_constraint(v, pltpu.HBM)
+            for v in (picks_of, cells_of, model_rows, sensitivity)
+        ],
+    )
+
+
 def local(model, sensitivity, pick_block, cell_block, blk_count, observed, pick_weight, station):
     shells, events = lax.axis_size("shells"), lax.axis_size("events")
     picks_of = pick_block.reshape(-1, LANES)
@@ -326,40 +355,12 @@
     stat_rows = STATIONS // LANES
     shape = jax.ShapeDtypeStruct
 
-    outside = pl.BlockSpec(memory_space=pltpu.HBM)
     lines, planes = torus_groups()
     devices = ("events", "shells")
 
     slots = sensitivity.shape[0]
     q = SLOT_CAP // 2
-    partials, blocks, codes = pl.pallas_call(
-        forward_kernel,
-        in_specs=[outside] * 5,
-        out_specs=(pl.BlockSpec(memory_space=pltpu.VMEM),) * 3,
-        out_shape=(
-            shape((shells, SLOT_CAP + 8, LANES), BF16),
-            shape(sensitivity.shape, BF16),
-            shape(picks_of.shape, jnp.int32),
-        ),
-        scratch_shapes=[
-            pltpu.SMEM((1,), jnp.int32),
-            pltpu.VMEM(picks_of.shape, jnp.int32),
-            pltpu.VMEM(cells_of.shape, jnp.int32),
-            pltpu.VMEM(model_rows.shape, BF16),
-            pltpu.VMEM((slots, 2 * LANES), BF16),
-            pltpu.VMEM((shells * q, slots), BF16),
-            pltpu.SemaphoreType.DMA((4,)),
-            pltpu.SemaphoreType.DMA((16,)),
-        ],
-        compiler_params=pltpu.CompilerParams(vmem_limit_bytes=VMEM_BYTES),
-        name="forward",
-    )(
-        blk_count,
-        *[
-            pltpu.with_memory_space_constraint(v, pltpu.HBM)
-            for v in (picks_of, cells_of, model_rows, sensitivity)
-        ],
-    )
+    partials, blocks, codes = forward_call(blk_count, picks_of, cells_of, model_rows, sensitivity, shells)
     partials = swap(partials, "shells")
     misfit, stats = simple(
         stations_kernel,
@@ -382,7 +383,6 @@
         "weighted",
     )(stats, misfit, weight, station, partials)
     halves = swap(halves, "shells").reshape(shells * q, LANES)
-    vmem = pl.BlockSpec(memory_space=pltpu.VMEM)
     grads, correction, weighted = simple(
         backward_kernel,
         (
@@ -391,7 +391,7 @@
             shape(weighted.shape, F32),
         ),
         "backward",
-        out_specs=(vmem, outside, outside),
+        out_specs=(INSIDE, OUTSIDE, OUTSIDE),
         scratch_shapes=[pltpu.VMEM((slots, 2 * LANES), BF16), pltpu.SemaphoreType.DMA((2,))],
     )(codes, cells_of, halves, blocks, correction, weighted)
     grads = swap(grads, "events")
@@ -399,7 +399,7 @@
         gradient_kernel,
         shape(model_rows.shape, F32),
         "gradient",
-        out_specs=outside,
+        out_specs=OUTSIDE,
         scratch_shapes=[pltpu.VMEM(model_rows.shape, F32), pltpu.SemaphoreType.DMA((4,))],
     )(grads)
     return (gradient.reshape(-1), correction.reshape(-1), weighted.reshape(-1))

time: 98.4 us -> 98 us (level)
  no operation moved by 1% of the time
where the time goes in v6:
time: 98 us; the launch traced here: 97.7 us
  blocking collectives  85.7 us (87%)
  Pallas kernels  10.6 us (11%)
  between operations  1.38 us (1%)
    all_to_all x5, blocking collectives, swap(): return lax.all_to_all(x, axis, 0, 0, tiled=True, axis_index_groups=groups)  85.7 us
    pallas_call x1, Pallas kernels, forward_call(): pl.pallas_call(forward_kernel, in_specs=[OUTSIDE] * 5, out_specs=(INSIDE,...  6.17 us
    pallas_call x1, Pallas kernels, local(): simple(backward_kernel, (shape((events,) + model_rows.shape, BF16), shape...  2.27 us

profile of v6, /device:TPU:1, one launch (start us, length us, event | category | flops | bytes accessed | tf_op | source)
XLA Modules:
  0.0 97.7 jit_solution(10248196052865928983)
XLA Ops:
  0.6 0.0 copy-start.3
  0.6 0.0 copy-start.1
  0.7 0.0 copy-start
  0.7 0.0 copy-start.2
  1.3 6.2 %forward.1 = (bf16[32,40,128]{2,1,0:T(8,128)(2,1)S(1)}, bf16[512,64,128]{2,1,0:T(8,128)(2,1)S(1)}, s32[4,128]{1,0:T(4,128)S(1)}) custom-call(s32[1]{0:T(128)S(6)} %copy.11.count_hbm, s32[4,128]{1,0:T(4,128)} %bitcast.20, s32[4,128]{1,0:T(4,128)} %bitcast.16, bf16[512,128]{1,0:T(8,128)(2,1)} %bitcast.19, bf16[512,64,128]{2,1,0:T(8,128)(2,1)} %blocks_hbm.1), custom_call_target="tpu_custom_call" | custom-call | tf_op jit(solution)/shard_map/forward/pallas_call | solution.py:317
  7.5 27.2 %all_to_all.25.terms_ref.partials_ref = bf16[32,40,128]{2,1,0:T(8,128)(2,1)S(1)} all-to-all(bf16[32,40,128]{2,1,0:T(8,128)(2,1)S(1)} %get-tuple-element.15), channel_id=1, replica_groups=mesh['events'=8,'shells'=32] {'shells'}, dimensions={0} | all-to-all | bytes 655360 | tf_op jit(solution)/shard_map/all_to_all | solution.py:303
  34.8 0.0 copy-done.1
  34.8 0.0 copy-done
  34.8 0.0 copy-done.2
  34.8 0.8 stations.1
  35.6 12.0 %all_to_all.26.terms_ref = f32[16,16,128]{2,1,0:T(8,128)S(1)} all-to-all(f32[16,16,128]{2,1,0:T(8,128)S(1)} %get-tuple-element.16), channel_id=1, replica_groups={{0,1,2,3,4,5,6,7,32,33,34,35,36,37,38,39},{8,9,10,11,12,13,14,15,40,41,..., dimensions={0} | all-to-all | bytes 262144 | tf_op jit(solution)/shard_map/all_to_all | solution.py:303
  47.7 14.0 %all_to_all.27.terms_ref = f32[32,16,128]{2,1,0:T(8,128)S(1)} all-to-all(f32[32,16,128]{2,1,0:T(8,128)S(1)} %spread.1), channel_id=1, replica_groups={{0,1,8,9,16,17,24,25,64,65,72,73,80,81,88,89,128,129,136,137,144,145,15..., dimensions={0} | all-to-all | bytes 524288 | tf_op jit(solution)/shard_map/all_to_all | solution.py:303
  61.6 0.5 weighted.1
  62.1 14.4 %all_to_all.28 = bf16[32,16,128]{2,1,0:T(8,128)(2,1)S(1)} all-to-all(bf16[32,16,128]{2,1,0:T(8,128)(2,1)S(1)} %get-tuple-element.18), channel_id=1, replica_groups=mesh['events'=8,'shells'=32] {'shells'}, dimensions={0} | all-to-all | bytes 262144 | tf_op jit(solution)/shard_map/all_to_all | solution.py:303
  76.5 0.0 copy-done.3
  76.5 2.3 %backward.1 = (bf16[8,512,128]{2,1,0:T(8,128)(2,1)S(1)}, f32[16,128]{1,0:T(8,128)}, f32[32,128]{1,0:T(8,128)}) custom-call(s32[4,128]{1,0:T(4,128)S(1)} %get-tuple-element.14.code_ref, s32[4,128]{1,0:T(4,128)S(1)} %bitcast.17, bf16[512,128]{1,0:T(8,128)(2,1)S(1)} %bitcast.10, bf16[512,64,128]{2,1,0:T(8,128)(2,1)S(1)} %get-tuple-element.19.blocks_ref, ...), custom_call_target="tpu_custom_call" | custom-call | tf_op jit(solution)/shard_map/backward/pallas_call | solution.py:386
  78.8 18.1 %all_to_all.29.terms_ref = bf16[8,512,128]{2,1,0:T(8,128)(2,1)S(1)} all-to-all(bf16[8,512,128]{2,1,0:T(8,128)(2,1)S(1)} %get-tuple-element.22), channel_id=1, replica_groups=mesh['events'=8,'shells'=32] {'events'}, dimensions={0} | all-to-all | bytes 2097152 | tf_op jit(solution)/shard_map/all_to_all | solution.py:303
  96.9 0.8 gradient.1
  (1 shorter events, 0.0 us)
Async XLA Ops:
  0.6 75.9 %copy-start.3 = (s32[512]{0:T(512)S(1)}, s32[512]{0:T(512)}, u32[]{:S(2)}) copy-start(s32[512]{0:T(512)} %param.11) | copy-start | bytes 6148
  0.6 34.1 %copy-start.1 = (s32[4096]{0:T(1024)S(1)}, s32[4096]{0:T(1024)}, u32[]{:S(2)}) copy-start(s32[4096]{0:T(1024)} %param.15) | copy-start | bytes 49156
  0.7 34.1 %copy-start = (f32[4096]{0:T(1024)S(1)}, f32[4096]{0:T(1024)}, u32[]{:S(2)}) copy-start(f32[4096]{0:T(1024)} %param.14) | copy-start | bytes 49156
  0.7 34.1 %copy-start.2 = (f32[4096]{0:T(1024)S(1)}, f32[4096]{0:T(1024)}, u32[]{:S(2)}) copy-start(f32[4096]{0:T(1024)} %param.13) | copy-start | bytes 49156

commit v7 on v6

--- a/solution.py
+++ b/solution.py
@@ -19,6 +19,7 @@
 TN = (((0,), (0,)), ((), ()))
 SLOT_CAP = 32
 VMEM_BYTES = 40 << 20
+PIECES = 4
 OUTSIDE = pl.BlockSpec(memory_space=pltpu.HBM)
 INSIDE = pl.BlockSpec(memory_space=pltpu.VMEM)
 
@@ -49,7 +50,7 @@
 
 
 def forward_kernel(count_hbm, pick_hbm, cell_hbm, model_hbm, blocks_hbm, out_ref, blocks_ref, code_ref,
-                   count, pick_ref, cell_ref, model_ref, values_ref, hot_ref, table_sems, block_sem):
+                   count, pick_ref, cell_ref, model_ref, values_ref, hot_ref, table_sems, block_sems):
     slots, cells = blocks_ref.shape[0], model_ref.shape[0]
     owners = out_ref.shape[0]
     chunks = range(slots // CHUNK)
@@ -61,8 +62,17 @@
     ]
     for copy in tables:
         copy.start()
-    block_copy = pltpu.make_async_copy(blocks_hbm, blocks_ref, block_sem)
-    block_copy.start()
+    piece = slots // block_sems.shape[0]
+
+    def block_copy(n):
+        at = pl.ds(n * piece, piece)
+        return pltpu.make_async_copy(blocks_hbm.at[at], blocks_ref.at[at], block_sems.at[n])
+
+    def start_copy(n, carry):
+        block_copy(n).start()
+        return carry
+
+    lax.fori_loop(0, slots // piece, start_copy, 0)
     for copy in tables:
         copy.wait()
     lane, sub = iota((CHUNK, LANES), 1), iota((CHUNK, LANES), 0)
@@ -98,11 +108,12 @@
     out_ref[:, SLOT_CAP:, :] = index.astype(BF16).reshape(owners, 8, LANES)
 
     lane_g, sub_g = iota((GROUP, LANES), 1), iota((GROUP, LANES), 0)
-    block_copy.wait()
     for n in chunks:
         parts = []
         for j in range(0, CHUNK, GROUP):
             first = n * CHUNK + j
+            if first % piece == 0:
+                block_copy(first // piece).wait()
             block = blocks_ref[first : first + GROUP].reshape(GROUP * PICK_BLK, CELL_BLK)
             wide = lax.dot_general(
                 rows[n][j : j + GROUP].astype(BF16), block, NT, preferred_element_type=F32
@@ -260,17 +271,22 @@
     cells_of = cell_ref[...]
     both = terms_ref[...]
     tile = 2 * LANES
-    for t in range(0, out_ref.shape[1], tile):
+    for t in range(0, out_ref.shape[0], tile):
         hot = jnp.concatenate(
             [pick(iota((tile, LANES), 0) + t == cells_of[r : r + 1]) for r in range(slots // LANES)],
             axis=1,
         )
         sums = jnp.dot(hot, both, preferred_element_type=F32)
         sums = (sums[:, :LANES] + sums[:, LANES:]).astype(BF16)
-        for s in range(out_ref.shape[0]):
-            out_ref[s, t : t + tile, :] = sums
+        out_ref[t : t + tile, :] = sums
     for copy in copies:
         copy.wait()
+
+
+def pair_kernel(own_ref, other_ref, out_ref):
+    total = (own_ref[...].astype(F32) + other_ref[...].astype(F32)).astype(BF16)
+    for s in range(out_ref.shape[0]):
+        out_ref[s] = total
 
 
 def gradient_kernel(terms_ref, out_hbm, total_ref, sems):
@@ -331,7 +347,7 @@
             pltpu.VMEM((slots, 2 * LANES), BF16),
             pltpu.VMEM((shells * SLOT_CAP // 2, slots), BF16),
             pltpu.SemaphoreType.DMA((4,)),
-            pltpu.SemaphoreType.DMA,
+            pltpu.SemaphoreType.DMA((PIECES,)),
         ],
         compiler_params=pltpu.CompilerParams(vmem_limit_bytes=VMEM_BYTES),
         name="forward",
@@ -386,7 +402,7 @@
     grads, correction, weighted = simple(
         backward_kernel,
         (
-            shape((events,) + model_rows.shape, BF16),
+            shape(model_rows.shape, BF16),
             shape(correction.shape, F32),
             shape(weighted.shape, F32),
         ),
@@ -394,7 +410,9 @@
         out_specs=(INSIDE, OUTSIDE, OUTSIDE),
         scratch_shapes=[pltpu.VMEM((slots, 2 * LANES), BF16), pltpu.SemaphoreType.DMA((2,))],
     )(codes, cells_of, halves, blocks, correction, weighted)
-    grads = swap(grads, "events")
+    other = lax.ppermute(grads, "events", [(e, e ^ 1) for e in range(events)])
+    grads = simple(pair_kernel, shape((events // 2,) + model_rows.shape, BF16), "pair")(grads, other)
+    grads = swap(grads, "events", [list(range(e, events, 2)) for e in (0, 1)])
     gradient = simple(
         gradient_kernel,
         shape(model_rows.shape, F32),

time: 98 us -> 94.7 us (0.966)
  blocking collectives: 85.7 us -> 78.6 us
  waiting for transfers between devices: 0 us -> 4.15 us
  Pallas kernels: 10.6 us -> 9.42 us
    all_to_all x5, blocking collectives: 85.7 us -> 78.6 us  [swap(): return lax.all_to_all(x, axis, 0, 0, tiled=True, axis_index_groups=groups)]
    ppermute x0 -> x1, waiting for transfers between devices: none -> 4.15 us  [local(): other = lax.ppermute(grads, 'events', [(e, e ^ 1) for e in range(events)])]
    pallas_call x1, Pallas kernels: 6.17 us -> 5.01 us  [forward_call(): pl.pallas_call(forward_kernel, in_specs=[OUTSIDE] * 5, out_specs=(INSIDE,...]
    pallas_call x1 -> x2, Pallas kernels: 2.27 us -> 2.29 us  [the longest x1 2.25 us: local(): simple(backward_kernel, (shape(model_rows.shape, BF16), shape(correction....]
  transfers between devices with their start and end apart: 0 -> 1, of which waited for: 0 -> 1; matrix products, arithmetic and copies ran while one was open for 0% -> 0% of each run, Pallas kernels for 0% -> 0%
where the time goes in v7:
time: 94.7 us; the launch traced here: 94.4 us
  blocking collectives  78.6 us (83%)
  Pallas kernels  9.42 us (10%)
  waiting for transfers between devices  4.15 us (4%)
  between operations  1.38 us (1%)
    all_to_all x5, blocking collectives, swap(): return lax.all_to_all(x, axis, 0, 0, tiled=True, axis_index_groups=groups)  78.6 us
    pallas_call x1, Pallas kernels, forward_call(): pl.pallas_call(forward_kernel, in_specs=[OUTSIDE] * 5, out_specs=(INSIDE,...  5.01 us
    ppermute x1, waiting for transfers between devices, local(): other = lax.ppermute(grads, 'events', [(e, e ^ 1) for e in range(events)])  4.15 us
    pallas_call x1, Pallas kernels, local(): simple(backward_kernel, (shape(model_rows.shape, BF16), shape(correction....  2.25 us
  transfers between devices with their start and end apart: 1, of which 1 were waited for; matrix products, arithmetic and copies ran while one was open for 0% of the time, Pallas kernels for 0%

profile of v7, /device:TPU:1, one launch (start us, length us, event | category | flops | bytes accessed | tf_op | source)
XLA Modules:
  0.0 94.4 jit_solution(12492091519238615358)
XLA Ops:
  0.6 0.0 copy-start.3
  0.6 0.0 copy-start.1
  0.7 0.0 copy-start
  0.7 0.0 copy-start.2
  1.3 5.0 %forward.1 = (bf16[32,40,128]{2,1,0:T(8,128)(2,1)S(1)}, bf16[512,64,128]{2,1,0:T(8,128)(2,1)S(1)}, s32[4,128]{1,0:T(4,128)S(1)}) custom-call(s32[1]{0:T(128)S(6)} %copy.11.count_hbm, s32[4,128]{1,0:T(4,128)} %bitcast.20, s32[4,128]{1,0:T(4,128)} %bitcast.16, bf16[512,128]{1,0:T(8,128)(2,1)} %bitcast.19, bf16[512,64,128]{2,1,0:T(8,128)(2,1)} %blocks_hbm.1), custom_call_target="tpu_custom_call" | custom-call | tf_op jit(solution)/shard_map/forward/pallas_call | solution.py:333
  6.4 27.3 %all_to_all.25.terms_ref.partials_ref = bf16[32,40,128]{2,1,0:T(8,128)(2,1)S(1)} all-to-all(bf16[32,40,128]{2,1,0:T(8,128)(2,1)S(1)} %get-tuple-element.15), channel_id=1, replica_groups=mesh['events'=8,'shells'=32] {'shells'}, dimensions={0} | all-to-all | bytes 655360 | tf_op jit(solution)/shard_map/all_to_all | solution.py:319
  33.6 0.0 copy-done.1
  33.6 0.0 copy-done
  33.6 0.0 copy-done.2
  33.6 0.8 stations.1
  34.5 12.0 %all_to_all.26.terms_ref = f32[16,16,128]{2,1,0:T(8,128)S(1)} all-to-all(f32[16,16,128]{2,1,0:T(8,128)S(1)} %get-tuple-element.16), channel_id=1, replica_groups={{0,1,2,3,4,5,6,7,32,33,34,35,36,37,38,39},{8,9,10,11,12,13,14,15,40,41,..., dimensions={0} | all-to-all | bytes 262144 | tf_op jit(solution)/shard_map/all_to_all | solution.py:319
  46.5 14.0 %all_to_all.27.terms_ref = f32[32,16,128]{2,1,0:T(8,128)S(1)} all-to-all(f32[32,16,128]{2,1,0:T(8,128)S(1)} %spread.1), channel_id=1, replica_groups={{0,1,8,9,16,17,24,25,64,65,72,73,80,81,88,89,128,129,136,137,144,145,15..., dimensions={0} | all-to-all | bytes 524288 | tf_op jit(solution)/shard_map/all_to_all | solution.py:319
  60.5 0.5 weighted.1
  61.0 14.4 %all_to_all.28 = bf16[32,16,128]{2,1,0:T(8,128)(2,1)S(1)} all-to-all(bf16[32,16,128]{2,1,0:T(8,128)(2,1)S(1)} %get-tuple-element.18), channel_id=1, replica_groups=mesh['events'=8,'shells'=32] {'shells'}, dimensions={0} | all-to-all | bytes 262144 | tf_op jit(solution)/shard_map/all_to_all | solution.py:319
  75.4 0.0 copy-done.3
  75.4 2.2 %backward.1 = (bf16[512,128]{1,0:T(8,128)(2,1)S(1)}, f32[16,128]{1,0:T(8,128)}, f32[32,128]{1,0:T(8,128)}) custom-call(s32[4,128]{1,0:T(4,128)S(1)} %get-tuple-element.14.code_ref, s32[4,128]{1,0:T(4,128)S(1)} %bitcast.17, bf16[512,128]{1,0:T(8,128)(2,1)S(1)} %bitcast.10, bf16[512,64,128]{2,1,0:T(8,128)(2,1)S(1)} %get-tuple-element.19.blocks_ref, ...), custom_call_target="tpu_custom_call" | custom-call | tf_op jit(solution)/shard_map/backward/pallas_call | solution.py:402
  77.6 0.9 collective-permute-start
  78.5 4.1 %collective-permute-done.other_ref = bf16[512,128]{1,0:T(8,128)(2,1)S(1)} collective-permute-done((bf16[512,128]{1,0:T(8,128)(2,1)S(1)}, bf16[512,128]{1,0:T(8,128)(2,1)S(1)}, u32[]{:S(2)}, u32[]{:S(2)}) %collective-permute-start) | collective-permute-done | bytes 131104 | tf_op jit(solution)/shard_map/ppermute | solution.py:413
  82.7 11.0 %all_to_all.29.terms_ref = bf16[4,512,128]{2,1,0:T(8,128)(2,1)S(1)} all-to-all(bf16[4,512,128]{2,1,0:T(8,128)(2,1)S(1)} %pair.1), channel_id=1, replica_groups={{0,64,128,192},{32,96,160,224},{1,65,129,193},{33,97,161,225},{2,66,130..., dimensions={0} | all-to-all | bytes 1048576 | tf_op jit(solution)/shard_map/all_to_all | solution.py:319
  93.7 0.7 gradient.1
  (2 shorter events, 0.1 us)
Async XLA Ops:
  0.6 74.7 %copy-start.3 = (s32[512]{0:T(512)S(1)}, s32[512]{0:T(512)}, u32[]{:S(2)}) copy-start(s32[512]{0:T(512)} %param.11) | copy-start | bytes 6148
  0.6 33.0 %copy-start.1 = (s32[4096]{0:T(1024)S(1)}, s32[4096]{0:T(1024)}, u32[]{:S(2)}) copy-start(s32[4096]{0:T(1024)} %param.15) | copy-start | bytes 49156
  0.7 33.0 %copy-start = (f32[4096]{0:T(1024)S(1)}, f32[4096]{0:T(1024)}, u32[]{:S(2)}) copy-start(f32[4096]{0:T(1024)} %param.14) | copy-start | bytes 49156
  0.7 33.0 %copy-start.2 = (f32[4096]{0:T(1024)S(1)}, f32[4096]{0:T(1024)}, u32[]{:S(2)}) copy-start(f32[4096]{0:T(1024)} %param.13) | copy-start | bytes 49156
  77.6 5.1 %collective-permute-start = (bf16[512,128]{1,0:T(8,128)(2,1)S(1)}, bf16[512,128]{1,0:T(8,128)(2,1)S(1)}, u32[]{:S(2)}, u32[]{:S(2)}) collective-permute-start(bf16[512,128]{1,0:T(8,128)(2,1)S(1)} %get-tuple-element.22.own_ref), channel_id=1, source_target_pairs={{0,32},{32,0},{64,96},{96,64},{128,160},{160,128},{192,224},{224,1... | collective-permute-start | bytes 393224 | tf_op jit(solution)/shard_map/ppermute | solution.py:413

commit v8 on v7

--- a/solution.py
+++ b/solution.py
@@ -231,7 +231,7 @@
 
 
 def backward_kernel(code_ref, cell_ref, resid_ref, blocks_ref, corr_ref, weighted_ref,
-                    out_ref, corr_hbm, weighted_hbm, terms_ref, sems):
+                    keep_ref, send_ref, corr_hbm, weighted_hbm, terms_ref, sems):
     copies = [
         pltpu.make_async_copy(corr_ref, corr_hbm, sems.at[0]),
         pltpu.make_async_copy(weighted_ref, weighted_hbm, sems.at[1]),
@@ -270,21 +270,21 @@
         terms_ref[n * CHUNK : (n + 1) * CHUNK, LANES : 2 * LANES] = low
     cells_of = cell_ref[...]
     both = terms_ref[...]
-    tile = 2 * LANES
-    for t in range(0, out_ref.shape[0], tile):
+    cells = keep_ref.shape[0]
+    parity = lax.axis_index("events") & 1
+    for ref, side in ((send_ref, 1 - parity), (keep_ref, parity)):
+        inside = cells_of - side * cells
         hot = jnp.concatenate(
-            [pick(iota((tile, LANES), 0) + t == cells_of[r : r + 1]) for r in range(slots // LANES)],
-            axis=1,
+            [pick(iota((cells, LANES), 0) == inside[r : r + 1]) for r in range(slots // LANES)], axis=1
         )
         sums = jnp.dot(hot, both, preferred_element_type=F32)
-        sums = (sums[:, :LANES] + sums[:, LANES:]).astype(BF16)
-        out_ref[t : t + tile, :] = sums
+        ref[...] = (sums[:, :LANES] + sums[:, LANES:]).astype(ref.dtype)
     for copy in copies:
         copy.wait()
 
 
 def pair_kernel(own_ref, other_ref, out_ref):
-    total = (own_ref[...].astype(F32) + other_ref[...].astype(F32)).astype(BF16)
+    total = (own_ref[...] + other_ref[...].astype(F32)).astype(BF16)
     for s in range(out_ref.shape[0]):
         out_ref[s] = total
 
@@ -294,10 +294,11 @@
     rows = total_ref.shape[0] // pieces
     copies = []
     for n in range(pieces):
+        side, start = divmod(n * rows, terms_ref.shape[1])
+        total = terms_ref[side, start : start + rows, :].astype(F32)
+        for s in range(side + 2, terms_ref.shape[0], 2):
+            total = total + terms_ref[s, start : start + rows, :].astype(F32)
         at = pl.ds(n * rows, rows)
-        total = terms_ref[0, at, :].astype(F32)
-        for s in range(1, terms_ref.shape[0]):
-            total = total + terms_ref[s, at, :].astype(F32)
         total_ref[at, :] = total
         copies.append(pltpu.make_async_copy(total_ref.at[at], out_hbm.at[at], sems.at[n]))
         copies[-1].start()
@@ -399,20 +400,22 @@
         "weighted",
     )(stats, misfit, weight, station, partials)
     halves = swap(halves, "shells").reshape(shells * q, LANES)
-    grads, correction, weighted = simple(
+    half_cells = (model_rows.shape[0] // 2, LANES)
+    kept, sent, correction, weighted = simple(
         backward_kernel,
         (
-            shape(model_rows.shape, BF16),
+            shape(half_cells, F32),
+            shape(half_cells, BF16),
             shape(correction.shape, F32),
             shape(weighted.shape, F32),
         ),
         "backward",
-        out_specs=(INSIDE, OUTSIDE, OUTSIDE),
+        out_specs=(INSIDE, INSIDE, OUTSIDE, OUTSIDE),
         scratch_shapes=[pltpu.VMEM((slots, 2 * LANES), BF16), pltpu.SemaphoreType.DMA((2,))],
     )(codes, cells_of, halves, blocks, correction, weighted)
-    other = lax.ppermute(grads, "events", [(e, e ^ 1) for e in range(events)])
-    grads = simple(pair_kernel, shape((events // 2,) + model_rows.shape, BF16), "pair")(grads, other)
-    grads = swap(grads, "events", [list(range(e, events, 2)) for e in (0, 1)])
+    other = lax.ppermute(sent, "events", [(e, e ^ 1) for e in range(events)])
+    grads = simple(pair_kernel, shape((events,) + half_cells, BF16), "pair")(kept, other)
+    grads = swap(grads, "events")
     gradient = simple(
         gradient_kernel,
         shape(model_rows.shape, F32),

time: 94.7 us -> 94.3 us (level)
  waiting for transfers between devices: 4.15 us -> 2.75 us
    ppermute x1, waiting for transfers between devices: 4.15 us -> 2.75 us  [local(): other = lax.ppermute(sent, 'events', [(e, e ^ 1) for e in range(events)])]
where the time goes in v8:
time: 94.3 us; the launch traced here: 94 us
  blocking collectives  79.3 us (84%)
  Pallas kernels  9.65 us (10%)
  waiting for transfers between devices  2.75 us (3%)
  between operations  1.38 us (1%)
    all_to_all x5, blocking collectives, swap(): return lax.all_to_all(x, axis, 0, 0, tiled=True, axis_index_groups=groups)  79.3 us
    pallas_call x1, Pallas kernels, forward_call(): pl.pallas_call(forward_kernel, in_specs=[OUTSIDE] * 5, out_specs=(INSIDE,...  5 us
    ppermute x1, waiting for transfers between devices, local(): other = lax.ppermute(sent, 'events', [(e, e ^ 1) for e in range(events)])  2.75 us
    pallas_call x1, Pallas kernels, local(): simple(backward_kernel, (shape(half_cells, F32), shape(half_cells, BF16),...  2.49 us
  transfers between devices with their start and end apart: 1, of which 1 were waited for; matrix products, arithmetic and copies ran while one was open for 0% of the time, Pallas kernels for 0%

profile of v8, /device:TPU:1, one launch (start us, length us, event | category | flops | bytes accessed | tf_op | source)
XLA Modules:
  0.0 94.0 jit_solution(9232082602611847299)
XLA Ops:
  0.6 0.0 copy-start.3
  0.6 0.0 copy-start.1
  0.7 0.0 copy-start
  0.7 0.0 copy-start.2
  1.3 5.0 %forward.1 = (bf16[32,40,128]{2,1,0:T(8,128)(2,1)S(1)}, bf16[512,64,128]{2,1,0:T(8,128)(2,1)S(1)}, s32[4,128]{1,0:T(4,128)S(1)}) custom-call(s32[1]{0:T(128)S(6)} %copy.11.count_hbm, s32[4,128]{1,0:T(4,128)} %bitcast.20, s32[4,128]{1,0:T(4,128)} %bitcast.16, bf16[512,128]{1,0:T(8,128)(2,1)} %bitcast.19, bf16[512,64,128]{2,1,0:T(8,128)(2,1)} %blocks_hbm.1), custom_call_target="tpu_custom_call" | custom-call | tf_op jit(solution)/shard_map/forward/pallas_call | solution.py:334
  6.4 27.3 %all_to_all.25.terms_ref.partials_ref = bf16[32,40,128]{2,1,0:T(8,128)(2,1)S(1)} all-to-all(bf16[32,40,128]{2,1,0:T(8,128)(2,1)S(1)} %get-tuple-element.16), channel_id=1, replica_groups=mesh['events'=8,'shells'=32] {'shells'}, dimensions={0} | all-to-all | bytes 655360 | tf_op jit(solution)/shard_map/all_to_all | solution.py:320
  33.6 0.0 copy-done.1
  33.6 0.0 copy-done
  33.6 0.0 copy-done.2
  33.6 0.8 stations.1
  34.5 12.0 %all_to_all.26.terms_ref = f32[16,16,128]{2,1,0:T(8,128)S(1)} all-to-all(f32[16,16,128]{2,1,0:T(8,128)S(1)} %get-tuple-element.17), channel_id=1, replica_groups={{0,1,2,3,4,5,6,7,32,33,34,35,36,37,38,39},{8,9,10,11,12,13,14,15,40,41,..., dimensions={0} | all-to-all | bytes 262144 | tf_op jit(solution)/shard_map/all_to_all | solution.py:320
  46.5 14.0 %all_to_all.27.terms_ref = f32[32,16,128]{2,1,0:T(8,128)S(1)} all-to-all(f32[32,16,128]{2,1,0:T(8,128)S(1)} %spread.1), channel_id=1, replica_groups={{0,1,8,9,16,17,24,25,64,65,72,73,80,81,88,89,128,129,136,137,144,145,15..., dimensions={0} | all-to-all | bytes 524288 | tf_op jit(solution)/shard_map/all_to_all | solution.py:320
  60.5 0.5 weighted.1
  61.0 14.4 %all_to_all.28 = bf16[32,16,128]{2,1,0:T(8,128)(2,1)S(1)} all-to-all(bf16[32,16,128]{2,1,0:T(8,128)(2,1)S(1)} %get-tuple-element.19), channel_id=1, replica_groups=mesh['events'=8,'shells'=32] {'shells'}, dimensions={0} | all-to-all | bytes 262144 | tf_op jit(solution)/shard_map/all_to_all | solution.py:320
  75.3 0.0 copy-done.3
  75.3 2.5 %backward.1 = (f32[256,128]{1,0:T(8,128)S(1)}, bf16[256,128]{1,0:T(8,128)(2,1)S(1)}, f32[16,128]{1,0:T(8,128)}, f32[32,128]{1,0:T(8,128)}) custom-call(s32[4,128]{1,0:T(4,128)S(1)} %get-tuple-element.15.code_ref, s32[4,128]{1,0:T(4,128)S(1)} %bitcast.17, bf16[512,128]{1,0:T(8,128)(2,1)S(1)} %bitcast.10, ...), custom_call_target="tpu_custom_call" | custom-call | tf_op jit(solution)/shard_map/backward/pallas_call | solution.py:404
  77.8 0.9 collective-permute-start
  78.7 2.7 %collective-permute-done.other_ref = bf16[256,128]{1,0:T(8,128)(2,1)S(1)} collective-permute-done((bf16[256,128]{1,0:T(8,128)(2,1)S(1)}, bf16[256,128]{1,0:T(8,128)(2,1)S(1)}, u32[]{:S(2)}, u32[]{:S(2)}) %collective-permute-start) | collective-permute-done | bytes 65568 | tf_op jit(solution)/shard_map/ppermute | solution.py:416
  81.5 11.7 %all_to_all.29.terms_ref = bf16[8,256,128]{2,1,0:T(8,128)(2,1)S(1)} all-to-all(bf16[8,256,128]{2,1,0:T(8,128)(2,1)S(1)} %pair.1), channel_id=1, replica_groups=mesh['events'=8,'shells'=32] {'events'}, dimensions={0} | all-to-all | bytes 1048576 | tf_op jit(solution)/shard_map/all_to_all | solution.py:320
  93.2 0.7 gradient.1
  (2 shorter events, 0.1 us)
Async XLA Ops:
  0.6 74.7 %copy-start.3 = (s32[512]{0:T(512)S(1)}, s32[512]{0:T(512)}, u32[]{:S(2)}) copy-start(s32[512]{0:T(512)} %param.11) | copy-start | bytes 6148
  0.6 33.0 %copy-start.1 = (s32[4096]{0:T(1024)S(1)}, s32[4096]{0:T(1024)}, u32[]{:S(2)}) copy-start(s32[4096]{0:T(1024)} %param.15) | copy-start | bytes 49156
  0.7 33.0 %copy-start = (f32[4096]{0:T(1024)S(1)}, f32[4096]{0:T(1024)}, u32[]{:S(2)}) copy-start(f32[4096]{0:T(1024)} %param.14) | copy-start | bytes 49156
  0.7 33.0 %copy-start.2 = (f32[4096]{0:T(1024)S(1)}, f32[4096]{0:T(1024)}, u32[]{:S(2)}) copy-start(f32[4096]{0:T(1024)} %param.13) | copy-start | bytes 49156
  77.8 3.7 %collective-permute-start = (bf16[256,128]{1,0:T(8,128)(2,1)S(1)}, bf16[256,128]{1,0:T(8,128)(2,1)S(1)}, u32[]{:S(2)}, u32[]{:S(2)}) collective-permute-start(bf16[256,128]{1,0:T(8,128)(2,1)S(1)} %get-tuple-element.24), channel_id=1, source_target_pairs={{0,32},{32,0},{64,96},{96,64},{128,160},{160,128},{192,224},{224,1... | collective-permute-start | bytes 196616 | tf_op jit(solution)/shard_map/ppermute | solution.py:416

commit v9 on v8

--- a/solution.py
+++ b/solution.py
@@ -49,7 +49,7 @@
     return high, mid, (rest - mid.astype(F32)).astype(BF16)
 
 
-def forward_kernel(count_hbm, pick_hbm, cell_hbm, model_hbm, blocks_hbm, out_ref, blocks_ref, code_ref,
+def forward_kernel(count_hbm, pick_hbm, cell_hbm, model_hbm, blocks_hbm, out_ref, blocks_ref, code_ref, side_ref,
                    count, pick_ref, cell_ref, model_ref, values_ref, hot_ref, table_sems, block_sems):
     slots, cells = blocks_ref.shape[0], model_ref.shape[0]
     owners = out_ref.shape[0]
@@ -77,6 +77,7 @@
         copy.wait()
     lane, sub = iota((CHUNK, LANES), 1), iota((CHUNK, LANES), 0)
     half = (lane >= PICK_BLK).astype(jnp.int32)
+    side_ref[...] = cell_ref[...] - (lax.axis_index("events") & 1) * (cells // 2)
 
     before, every = pick(sub < lane), jnp.ones((CHUNK, LANES), BF16)
     seen = jnp.zeros((owners, LANES), F32)
@@ -184,23 +185,31 @@
     h = hi_count
     numer = total[0:h] + total[h : 2 * h] + total[2 * h : 3 * h]
     denom = total[3 * h : 4 * h] + total[4 * h : 5 * h] + total[5 * h : 6 * h]
+    for first in (0, 1):
+        part = slice(first * h // 2, (first + 1) * h // 2)
+        sums = jnp.concatenate([p.astype(F32) for p in two_parts(numer[part])] + [denom[part]], axis=0)
+        for s in range(first, out_ref.shape[0], 2):
+            out_ref[s] = sums.astype(BF16)
+
+
+def spread_kernel(terms_ref, out_ref):
+    total = terms_ref[0].astype(F32)
+    for s in range(1, terms_ref.shape[0]):
+        total = total + terms_ref[s].astype(F32)
+    h = total.shape[0] // 3
+    sums = jnp.concatenate([total[:h] + total[h : 2 * h], total[2 * h :]], axis=0)
     for s in range(out_ref.shape[0]):
-        out_ref[s] = denom if s % 2 else numer
-
-
-def spread_kernel(terms_ref, out_ref):
-    total = terms_ref[0]
-    for s in range(1, terms_ref.shape[0]):
-        total = total + terms_ref[s]
-    for s in range(out_ref.shape[0]):
-        out_ref[s] = total
+        out_ref[s] = sums
 
 
 def weighted_kernel(terms_ref, misfit_ref, weight_ref, station_ref, partials_ref, corr_ref, weighted_ref, out_ref):
-    numer, denom = terms_ref[0], terms_ref[1]
+    lower, upper = terms_ref[0], terms_ref[1]
     for s in range(2, terms_ref.shape[0], 2):
-        numer = numer + terms_ref[s]
-        denom = denom + terms_ref[s + 1]
+        lower = lower + terms_ref[s]
+        upper = upper + terms_ref[s + 1]
+    h = lower.shape[0] // 2
+    numer = jnp.concatenate([lower[:h], upper[:h]], axis=0)
+    denom = jnp.concatenate([lower[h:], upper[h:]], axis=0)
     corr = numer / (denom + 1.0)
     corr_ref[...] = corr
     stations = station_ref[...]
@@ -268,14 +277,13 @@
         high, low = two_parts(jnp.concatenate(parts, axis=0))
         terms_ref[n * CHUNK : (n + 1) * CHUNK, 0:LANES] = high
         terms_ref[n * CHUNK : (n + 1) * CHUNK, LANES : 2 * LANES] = low
-    cells_of = cell_ref[...]
+    inside = cell_ref[...]
     both = terms_ref[...]
     cells = keep_ref.shape[0]
-    parity = lax.axis_index("events") & 1
-    for ref, side in ((send_ref, 1 - parity), (keep_ref, parity)):
-        inside = cells_of - side * cells
+    kept = jnp.logical_and(inside >= 0, inside < cells)
+    for ref, rows in ((send_ref, jnp.where(kept, -1, inside & (cells - 1))), (keep_ref, inside)):
         hot = jnp.concatenate(
-            [pick(iota((cells, LANES), 0) == inside[r : r + 1]) for r in range(slots // LANES)], axis=1
+            [pick(iota((cells, LANES), 0) == rows[r : r + 1]) for r in range(slots // LANES)], axis=1
         )
         sums = jnp.dot(hot, both, preferred_element_type=F32)
         ref[...] = (sums[:, :LANES] + sums[:, LANES:]).astype(ref.dtype)
@@ -334,11 +342,12 @@
     return pl.pallas_call(
         forward_kernel,
         in_specs=[OUTSIDE] * 5,
-        out_specs=(INSIDE,) * 3,
+        out_specs=(INSIDE,) * 4,
         out_shape=(
             jax.ShapeDtypeStruct((shells, SLOT_CAP + 8, LANES), BF16),
             jax.ShapeDtypeStruct(sensitivity.shape, BF16),
             jax.ShapeDtypeStruct(picks_of.shape, jnp.int32),
+            jax.ShapeDtypeStruct(cells_of.shape, jnp.int32),
         ),
         scratch_shapes=[
             pltpu.SMEM((1,), jnp.int32),
@@ -377,13 +386,13 @@
 
     slots = sensitivity.shape[0]
     q = SLOT_CAP // 2
-    partials, blocks, codes = forward_call(blk_count, picks_of, cells_of, model_rows, sensitivity, shells)
+    partials, blocks, codes, sides = forward_call(blk_count, picks_of, cells_of, model_rows, sensitivity, shells)
     partials = swap(partials, "shells")
     misfit, stats = simple(
         stations_kernel,
         (
             shape((own_rows, LANES), F32),
-            shape((len(lines[0]), stat_rows, LANES), F32),
+            shape((len(lines[0]), 3 * stat_rows // 2, LANES), BF16),
         ),
         "stations",
     )(partials, observed, weight, station)
@@ -412,7 +421,7 @@
         "backward",
         out_specs=(INSIDE, INSIDE, OUTSIDE, OUTSIDE),
         scratch_shapes=[pltpu.VMEM((slots, 2 * LANES), BF16), pltpu.SemaphoreType.DMA((2,))],
-    )(codes, cells_of, halves, blocks, correction, weighted)
+    )(codes, sides, halves, blocks, correction, weighted)
     other = lax.ppermute(sent, "events", [(e, e ^ 1) for e in range(events)])
     grads = simple(pair_kernel, shape((events,) + half_cells, BF16), "pair")(kept, other)
     grads = swap(grads, "events")

time: 94.3 us -> 93.3 us (0.989)
  no operation moved by 1% of the time
where the time goes in v9:
time: 93.3 us; the launch traced here: 93 us
  blocking collectives  78.6 us (84%)
  Pallas kernels  9.41 us (10%)
  waiting for transfers between devices  2.81 us (3%)
  between operations  1.37 us (1%)
    all_to_all x5, blocking collectives, swap(): return lax.all_to_all(x, axis, 0, 0, tiled=True, axis_index_groups=groups)  78.6 us
    pallas_call x1, Pallas kernels, forward_call(): pl.pallas_call(forward_kernel, in_specs=[OUTSIDE] * 5, out_specs=(INSIDE,...  5 us
    ppermute x1, waiting for transfers between devices, local(): other = lax.ppermute(sent, 'events', [(e, e ^ 1) for e in range(events)])  2.81 us
    pallas_call x1, Pallas kernels, local(): simple(backward_kernel, (shape(half_cells, F32), shape(half_cells, BF16),...  2.24 us
  transfers between devices with their start and end apart: 1, of which 1 were waited for; matrix products, arithmetic and copies ran while one was open for 0% of the time, Pallas kernels for 0%

profile of v9, /device:TPU:1, one launch (start us, length us, event | category | flops | bytes accessed | tf_op | source)
XLA Modules:
  0.0 93.0 jit_solution(12754828348664343432)
XLA Ops:
  0.6 0.0 copy-start.1
  0.6 0.0 copy-start
  0.7 0.0 copy-start.2
  1.3 5.0 %forward.1 = (bf16[32,40,128]{2,1,0:T(8,128)(2,1)S(1)}, bf16[512,64,128]{2,1,0:T(8,128)(2,1)S(1)}, s32[4,128]{1,0:T(4,128)S(1)}, s32[4,128]{1,0:T(4,128)S(1)}) custom-call(s32[1]{0:T(128)S(6)} %copy.11.count_hbm, s32[4,128]{1,0:T(4,128)} %bitcast.18, s32[4,128]{1,0:T(4,128)} %bitcast.19, bf16[512,128]{1,0:T(8,128)(2,1)} %bitcast.17, ...), custom_call_target="tpu_custom_call" | custom-call | tf_op jit(solution)/shard_map/forward/pallas_call | solution.py:342
  6.3 27.3 %all_to_all.25.terms_ref.partials_ref = bf16[32,40,128]{2,1,0:T(8,128)(2,1)S(1)} all-to-all(bf16[32,40,128]{2,1,0:T(8,128)(2,1)S(1)} %get-tuple-element.18), channel_id=1, replica_groups=mesh['events'=8,'shells'=32] {'shells'}, dimensions={0} | all-to-all | bytes 655360 | tf_op jit(solution)/shard_map/all_to_all | solution.py:328
  33.6 0.0 copy-done.1
  33.6 0.0 copy-done
  33.6 0.0 copy-done.2
  33.6 0.8 stations.1
  34.5 11.3 %all_to_all.26.terms_ref = bf16[16,24,128]{2,1,0:T(8,128)(2,1)S(1)} all-to-all(bf16[16,24,128]{2,1,0:T(8,128)(2,1)S(1)} %get-tuple-element.19), channel_id=1, replica_groups={{0,1,2,3,4,5,6,7,32,33,34,35,36,37,38,39},{8,9,10,11,12,13,14,15,40,41,..., dimensions={0} | all-to-all | bytes 196608 | tf_op jit(solution)/shard_map/all_to_all | solution.py:328
  45.8 14.0 %all_to_all.27.terms_ref = f32[32,16,128]{2,1,0:T(8,128)S(1)} all-to-all(f32[32,16,128]{2,1,0:T(8,128)S(1)} %spread.1), channel_id=1, replica_groups={{0,1,8,9,16,17,24,25,64,65,72,73,80,81,88,89,128,129,136,137,144,145,15..., dimensions={0} | all-to-all | bytes 524288 | tf_op jit(solution)/shard_map/all_to_all | solution.py:328
  59.8 0.5 weighted.1
  60.3 14.4 %all_to_all.28 = bf16[32,16,128]{2,1,0:T(8,128)(2,1)S(1)} all-to-all(bf16[32,16,128]{2,1,0:T(8,128)(2,1)S(1)} %get-tuple-element.21), channel_id=1, replica_groups=mesh['events'=8,'shells'=32] {'shells'}, dimensions={0} | all-to-all | bytes 262144 | tf_op jit(solution)/shard_map/all_to_all | solution.py:328
  74.7 2.2 %backward.1 = (f32[256,128]{1,0:T(8,128)S(1)}, bf16[256,128]{1,0:T(8,128)(2,1)S(1)}, f32[16,128]{1,0:T(8,128)}, f32[32,128]{1,0:T(8,128)}) custom-call(s32[4,128]{1,0:T(4,128)S(1)} %get-tuple-element.16.code_ref, s32[4,128]{1,0:T(4,128)S(1)} %get-tuple-element.17.cell_ref, bf16[512,128]{1,0:T(8,128)(2,1)S(1)} %bitcast.10, ...), custom_call_target="tpu_custom_call" | custom-call | tf_op jit(solution)/shard_map/backward/pallas_call | solution.py:413
  77.0 0.8 collective-permute-start
  77.8 2.8 %collective-permute-done.other_ref = bf16[256,128]{1,0:T(8,128)(2,1)S(1)} collective-permute-done((bf16[256,128]{1,0:T(8,128)(2,1)S(1)}, bf16[256,128]{1,0:T(8,128)(2,1)S(1)}, u32[]{:S(2)}, u32[]{:S(2)}) %collective-permute-start) | collective-permute-done | bytes 65568 | tf_op jit(solution)/shard_map/ppermute | solution.py:425
  80.6 11.6 %all_to_all.29.terms_ref = bf16[8,256,128]{2,1,0:T(8,128)(2,1)S(1)} all-to-all(bf16[8,256,128]{2,1,0:T(8,128)(2,1)S(1)} %pair.1), channel_id=1, replica_groups=mesh['events'=8,'shells'=32] {'events'}, dimensions={0} | all-to-all | bytes 1048576 | tf_op jit(solution)/shard_map/all_to_all | solution.py:328
  92.3 0.7 gradient.1
  (2 shorter events, 0.1 us)
Async XLA Ops:
  0.6 33.0 %copy-start.1 = (s32[4096]{0:T(1024)S(1)}, s32[4096]{0:T(1024)}, u32[]{:S(2)}) copy-start(s32[4096]{0:T(1024)} %param.15) | copy-start | bytes 49156
  0.6 33.0 %copy-start = (f32[4096]{0:T(1024)S(1)}, f32[4096]{0:T(1024)}, u32[]{:S(2)}) copy-start(f32[4096]{0:T(1024)} %param.14) | copy-start | bytes 49156
  0.7 32.9 %copy-start.2 = (f32[4096]{0:T(1024)S(1)}, f32[4096]{0:T(1024)}, u32[]{:S(2)}) copy-start(f32[4096]{0:T(1024)} %param.13) | copy-start | bytes 49156
  77.0 3.6 %collective-permute-start = (bf16[256,128]{1,0:T(8,128)(2,1)S(1)}, bf16[256,128]{1,0:T(8,128)(2,1)S(1)}, u32[]{:S(2)}, u32[]{:S(2)}) collective-permute-start(bf16[256,128]{1,0:T(8,128)(2,1)S(1)} %get-tuple-element.26), channel_id=1, source_target_pairs={{0,32},{32,0},{64,96},{96,64},{128,160},{160,128},{192,224},{224,1... | collective-permute-start | bytes 196616 | tf_op jit(solution)/shard_map/ppermute | solution.py:425

commit v10 on v9

--- a/solution.py
+++ b/solution.py
@@ -40,13 +40,6 @@
 def two_parts(x):
     high = x.astype(BF16)
     return high, (x - high.astype(F32)).astype(BF16)
-
-
-def three_parts(x):
-    high, rest = x.astype(BF16), x
-    rest = x - high.astype(F32)
-    mid = rest.astype(BF16)
-    return high, mid, (rest - mid.astype(F32)).astype(BF16)
 
 
 def forward_kernel(count_hbm, pick_hbm, cell_hbm, model_hbm, blocks_hbm, out_ref, blocks_ref, code_ref, side_ref,
@@ -169,7 +162,7 @@
     stations = station_ref[...]
     high, low = stations >> 7, stations & (LANES - 1)
     hi_count = STATIONS // LANES
-    pieces = [p.astype(F32) for p in three_parts(weight * misfit) + three_parts(weight)]
+    pieces = [p.astype(F32) for p in two_parts(weight * misfit) + two_parts(weight)]
     total = jnp.zeros((len(pieces) * hi_count, LANES), F32)
     for r0 in range(0, rows, 8):
         left, right = [], []
@@ -183,8 +176,8 @@
             jnp.concatenate(left, axis=1), jnp.concatenate(right, axis=1), NT, preferred_element_type=F32
         )
     h = hi_count
-    numer = total[0:h] + total[h : 2 * h] + total[2 * h : 3 * h]
-    denom = total[3 * h : 4 * h] + total[4 * h : 5 * h] + total[5 * h : 6 * h]
+    numer = total[0:h] + total[h : 2 * h]
+    denom = total[2 * h : 3 * h] + total[3 * h : 4 * h]
     for first in (0, 1):
         part = slice(first * h // 2, (first + 1) * h // 2)
         sums = jnp.concatenate([p.astype(F32) for p in two_parts(numer[part])] + [denom[part]], axis=0)

time: 93.3 us -> 93.3 us (level)
  no operation moved by 1% of the time
where the time goes in v10:
time: 93.3 us; the launch traced here: 93 us
  blocking collectives  78.6 us (84%)
  Pallas kernels  9.41 us (10%)
  waiting for transfers between devices  2.79 us (3%)
  between operations  1.37 us (1%)
    all_to_all x5, blocking collectives, swap(): return lax.all_to_all(x, axis, 0, 0, tiled=True, axis_index_groups=groups)  78.6 us
    pallas_call x1, Pallas kernels, forward_call(): pl.pallas_call(forward_kernel, in_specs=[OUTSIDE] * 5, out_specs=(INSIDE,...  5 us
    ppermute x1, waiting for transfers between devices, local(): other = lax.ppermute(sent, 'events', [(e, e ^ 1) for e in range(events)])  2.79 us
    pallas_call x1, Pallas kernels, local(): simple(backward_kernel, (shape(half_cells, F32), shape(half_cells, BF16),...  2.24 us
  transfers between devices with their start and end apart: 1, of which 1 were waited for; matrix products, arithmetic and copies ran while one was open for 0% of the time, Pallas kernels for 0%

profile of v10, /device:TPU:1, one launch (start us, length us, event | category | flops | bytes accessed | tf_op | source)
XLA Modules:
  0.0 93.0 jit_solution(3390827484818917923)
XLA Ops:
  0.6 0.0 copy-start.1
  0.6 0.0 copy-start
  0.7 0.0 copy-start.2
  1.3 5.0 %forward.1 = (bf16[32,40,128]{2,1,0:T(8,128)(2,1)S(1)}, bf16[512,64,128]{2,1,0:T(8,128)(2,1)S(1)}, s32[4,128]{1,0:T(4,128)S(1)}, s32[4,128]{1,0:T(4,128)S(1)}) custom-call(s32[1]{0:T(128)S(6)} %copy.11.count_hbm, s32[4,128]{1,0:T(4,128)} %bitcast.18, s32[4,128]{1,0:T(4,128)} %bitcast.19, bf16[512,128]{1,0:T(8,128)(2,1)} %bitcast.17, ...), custom_call_target="tpu_custom_call" | custom-call | tf_op jit(solution)/shard_map/forward/pallas_call | solution.py:335
  6.3 27.3 %all_to_all.25.terms_ref.partials_ref = bf16[32,40,128]{2,1,0:T(8,128)(2,1)S(1)} all-to-all(bf16[32,40,128]{2,1,0:T(8,128)(2,1)S(1)} %get-tuple-element.18), channel_id=1, replica_groups=mesh['events'=8,'shells'=32] {'shells'}, dimensions={0} | all-to-all | bytes 655360 | tf_op jit(solution)/shard_map/all_to_all | solution.py:321
  33.6 0.0 copy-done.1
  33.6 0.0 copy-done
  33.6 0.0 copy-done.2
  33.6 0.8 stations.1
  34.5 11.3 %all_to_all.26.terms_ref = bf16[16,24,128]{2,1,0:T(8,128)(2,1)S(1)} all-to-all(bf16[16,24,128]{2,1,0:T(8,128)(2,1)S(1)} %get-tuple-element.19), channel_id=1, replica_groups={{0,1,2,3,4,5,6,7,32,33,34,35,36,37,38,39},{8,9,10,11,12,13,14,15,40,41,..., dimensions={0} | all-to-all | bytes 196608 | tf_op jit(solution)/shard_map/all_to_all | solution.py:321
  45.8 14.0 %all_to_all.27.terms_ref = f32[32,16,128]{2,1,0:T(8,128)S(1)} all-to-all(f32[32,16,128]{2,1,0:T(8,128)S(1)} %spread.1), channel_id=1, replica_groups={{0,1,8,9,16,17,24,25,64,65,72,73,80,81,88,89,128,129,136,137,144,145,15..., dimensions={0} | all-to-all | bytes 524288 | tf_op jit(solution)/shard_map/all_to_all | solution.py:321
  59.8 0.5 weighted.1
  60.3 14.4 %all_to_all.28 = bf16[32,16,128]{2,1,0:T(8,128)(2,1)S(1)} all-to-all(bf16[32,16,128]{2,1,0:T(8,128)(2,1)S(1)} %get-tuple-element.21), channel_id=1, replica_groups=mesh['events'=8,'shells'=32] {'shells'}, dimensions={0} | all-to-all | bytes 262144 | tf_op jit(solution)/shard_map/all_to_all | solution.py:321
  74.7 2.2 %backward.1 = (f32[256,128]{1,0:T(8,128)S(1)}, bf16[256,128]{1,0:T(8,128)(2,1)S(1)}, f32[16,128]{1,0:T(8,128)}, f32[32,128]{1,0:T(8,128)}) custom-call(s32[4,128]{1,0:T(4,128)S(1)} %get-tuple-element.16.code_ref, s32[4,128]{1,0:T(4,128)S(1)} %get-tuple-element.17.cell_ref, bf16[512,128]{1,0:T(8,128)(2,1)S(1)} %bitcast.10, ...), custom_call_target="tpu_custom_call" | custom-call | tf_op jit(solution)/shard_map/backward/pallas_call | solution.py:406
  77.0 0.8 collective-permute-start
  77.8 2.8 %collective-permute-done.other_ref = bf16[256,128]{1,0:T(8,128)(2,1)S(1)} collective-permute-done((bf16[256,128]{1,0:T(8,128)(2,1)S(1)}, bf16[256,128]{1,0:T(8,128)(2,1)S(1)}, u32[]{:S(2)}, u32[]{:S(2)}) %collective-permute-start) | collective-permute-done | bytes 65568 | tf_op jit(solution)/shard_map/ppermute | solution.py:418
  80.6 11.6 %all_to_all.29.terms_ref = bf16[8,256,128]{2,1,0:T(8,128)(2,1)S(1)} all-to-all(bf16[8,256,128]{2,1,0:T(8,128)(2,1)S(1)} %pair.1), channel_id=1, replica_groups=mesh['events'=8,'shells'=32] {'events'}, dimensions={0} | all-to-all | bytes 1048576 | tf_op jit(solution)/shard_map/all_to_all | solution.py:321
  92.3 0.7 gradient.1
  (2 shorter events, 0.1 us)
Async XLA Ops:
  0.6 33.0 %copy-start.1 = (s32[4096]{0:T(1024)S(1)}, s32[4096]{0:T(1024)}, u32[]{:S(2)}) copy-start(s32[4096]{0:T(1024)} %param.15) | copy-start | bytes 49156
  0.6 33.0 %copy-start = (f32[4096]{0:T(1024)S(1)}, f32[4096]{0:T(1024)}, u32[]{:S(2)}) copy-start(f32[4096]{0:T(1024)} %param.14) | copy-start | bytes 49156
  0.7 32.9 %copy-start.2 = (f32[4096]{0:T(1024)S(1)}, f32[4096]{0:T(1024)}, u32[]{:S(2)}) copy-start(f32[4096]{0:T(1024)} %param.13) | copy-start | bytes 49156
  77.0 3.6 %collective-permute-start = (bf16[256,128]{1,0:T(8,128)(2,1)S(1)}, bf16[256,128]{1,0:T(8,128)(2,1)S(1)}, u32[]{:S(2)}, u32[]{:S(2)}) collective-permute-start(bf16[256,128]{1,0:T(8,128)(2,1)S(1)} %get-tuple-element.26), channel_id=1, source_target_pairs={{0,32},{32,0},{64,96},{96,64},{128,160},{160,128},{192,224},{224,1... | collective-permute-start | bytes 196616 | tf_op jit(solution)/shard_map/ppermute | solution.py:418
